TPU v7x, 512 devices: a whole 4x4x16 slice. The times are simulated.
512 devices in a mesh: row: 32 (over x, y, core), col: 16 (over z).
Axes of the slice: x: 4, y: 4, z: 16, core: 2. Of those that a mesh axis runs over, the one named last changes fastest.
Arguments:
- tokens: bfloat16 [4096, 2560], P('row', 'col'), may hold values from -6 to 6
- w_gate: bfloat16 [512, 192, 2560], P(('row', 'col')), may hold values from -0.125 to 0.125
- w_up: bfloat16 [512, 192, 2560], P(('row', 'col')), may hold values from -0.125 to 0.125
- w_down: bfloat16 [512, 192, 2560], P(('row', 'col')), may hold values from -0.15625 to 0.15625
- adp_down: bfloat16 [64, 16, 2560], P('row', None, 'col'), may hold values from -0.125 to 0.125
- adp_up: bfloat16 [64, 16, 2560], P('row', None, 'col'), may hold values from -1.5 to 1.5
- expert_ids: int32 [4096, 6], P('row'), may hold values from 0 to 63, all different within a row; in each aligned block of 128 rows (0 to 127, 128 to 255, ...) at most 16 rows name the same one
- gate_vals: float32 [4096, 6], P('row'), may hold values from 0.05 to 0.5
- lengths: int32 [16], replicated, may hold values from 1 to 1365, 4096 in all
- perm: int32 [4096], P('row'), may hold values from 0 to 4095, each once
- req_adapter: int32 [16], replicated, may hold values from 0 to 63
Outputs:
- layer_out: bfloat16 [4096, 2560], P('row', 'col')
Inputs may be any that keep to these rules, and one draw needn't show every extreme that they name: `expert_ids`: within the 128 rows of one index of row, no expert is named by more than 16 rows, a bound that some block reaches; each row names 6 different experts. `perm`: each position appears once. `lengths`: they sum to 4096; the longest is exactly 4096 // 3.
All inputs are finite; a program needn't handle non-finite values.
Results may differ from a plain program's by a relative error of at most 0.0051.
Values may be sent and summed in bfloat16 or wider, within the bound.
A program may use at most 128 MiB of HBM per device.

v0:
```python
import jax
import jax.numpy as jnp
from jax import lax
from jax.sharding import PartitionSpec as P

adapter_scale_factor = 2.0


def contract_last(left, right):
    return lax.dot_general(
        left, right, (((1,), (1,)), ((), ())), preferred_element_type=jnp.float32
    )


def body(
    tokens,
    w_gate,
    w_up,
    w_down,
    adp_down,
    adp_up,
    expert_ids,
    gate_vals,
    lengths,
    perm,
    req_adapter,
):
    count_tok = tokens.shape[0]
    share = tokens.shape[1]
    rows_count = lax.axis_size("row")
    cols_count = lax.axis_size("col")
    experts = 2 * rows_count
    parts = cols_count // 2
    which = lax.axis_index("col") // parts
    topk = expert_ids.shape[1]
    capacity = max(2, (4 * count_tok * topk + 3 * experts - 1) // (3 * experts))
    weight_gate = w_gate[0]
    weight_up = w_up[0]
    down_projection_weight = w_down[0]
    flat_ids = expert_ids.reshape(-1)
    onehot = (flat_ids[:, None] == jnp.arange(experts, dtype=jnp.int32)[None, :]).astype(jnp.int32)
    slot = jnp.sum(onehot * jnp.cumsum(onehot, axis=0), axis=1) - 1
    place = (flat_ids * capacity + slot).reshape(count_tok, topk)
    targets = jnp.arange(experts * capacity, dtype=jnp.int32)
    dispatch = jnp.any(targets[:, None, None] == place[None, :, :], axis=2).astype(jnp.bfloat16)
    combine = jnp.sum(
        jnp.where(
            place[:, :, None] == targets[None, None, :], gate_vals[:, :, None], jnp.float32(0.0)
        ),
        axis=1,
    )
    outgoing = jnp.dot(dispatch, tokens, preferred_element_type=jnp.float32).astype(jnp.bfloat16)
    outgoing = outgoing.reshape(rows_count, 2, capacity, share)
    arrival_rows = lax.all_to_all(outgoing, "row", split_axis=0, concat_axis=0, tiled=True)
    piece = lax.all_gather(arrival_rows, "col", axis=3, tiled=True)
    cols = piece.shape[3]
    mine = lax.dynamic_index_in_dim(piece, which, 1, keepdims=False).reshape(
        rows_count * capacity, cols
    )
    gate = contract_last(mine, weight_gate)
    upper = contract_last(mine, weight_up)
    hidden = (jax.nn.silu(gate) * upper).astype(jnp.bfloat16)
    partial_out = jnp.dot(
        hidden, down_projection_weight, preferred_element_type=jnp.float32
    ).astype(jnp.bfloat16)
    pieces = partial_out.reshape(rows_count * capacity, cols_count, share)
    received = lax.all_to_all(pieces, "col", split_axis=1, concat_axis=1, tiled=True)
    summed = jnp.sum(
        received.astype(jnp.float32).reshape(rows_count, capacity, 2, parts, share), axis=3
    )
    summed = summed.transpose(0, 2, 1, 3)
    returned = lax.all_to_all(summed, "row", split_axis=0, concat_axis=0, tiled=True)
    dispatched_tokens = jnp.dot(
        combine, returned.reshape(experts * capacity, share), precision=lax.Precision.HIGHEST
    )
    down_all, up_all = (
        lax.all_gather(adp_down, "row", axis=0, tiled=True),
        lax.all_gather(adp_up, "row", axis=0, tiled=True),
    )
    adapters = down_all.shape[0]
    rank = down_all.shape[1]
    nreq = lengths.shape[0]
    ends = jnp.cumsum(lengths)
    request = jnp.sum((perm[:, None] >= ends[None, :]).astype(jnp.int32), axis=1)
    adapter = jnp.sum(
        jnp.where(
            request[:, None] == jnp.arange(nreq, dtype=jnp.int32)[None, :], req_adapter[None, :], 0
        ),
        axis=1,
    )
    onehot_a = (adapter[:, None] == jnp.arange(adapters, dtype=jnp.int32)[None, :]).astype(
        jnp.float32
    )
    projected = jnp.einsum(
        "td,kd->tk",
        tokens,
        down_all.reshape(adapters * rank, share),
        preferred_element_type=jnp.float32,
    )
    partial_low = jnp.sum(
        projected.reshape(count_tok, adapters, rank) * onehot_a[:, :, None], axis=1
    )
    low = lax.psum(partial_low, "col").astype(jnp.bfloat16)
    expanded = (onehot_a.astype(jnp.bfloat16)[:, :, None] * low[:, None, :]).reshape(
        count_tok, adapters * rank
    )
    adapter_update = jnp.dot(
        expanded, up_all.reshape(adapters * rank, share), preferred_element_type=jnp.float32
    )
    return (dispatched_tokens + adapter_scale_factor * adapter_update).astype(jnp.bfloat16)


def solution(mesh):
    in_specs = (
        P("row", "col"),
        P(("row", "col"), None, None),
        P(("row", "col"), None, None),
        P(("row", "col"), None, None),
        P("row", None, "col"),
        P("row", None, "col"),
        P("row", None),
        P("row", None),
        P(),
        P("row"),
        P(),
    )
    out_specs = P("row", "col")
    return jax.shard_map(body, mesh=mesh, in_specs=in_specs, out_specs=out_specs, check_vma=False)
```

profile of v0, /device:TPU:1, one launch (start us, length us, event | category | flops | bytes accessed | tf_op | source)
XLA Modules:
  0.0 505.6 jit_solution(4456110021463680649)
XLA Ops:
  6.5 0.0 copy-start
  6.5 0.0 all-gather.2.cloned.1.call-start
  6.5 0.9 copy.72
  7.4 0.1 eq.88
  7.6 0.1 eq.84
  7.7 1.8 reduce-window.18
  9.5 0.3 slice_reduce_fusion
  9.8 0.1 fusion.20
  10.0 0.1 sub.11
  10.1 0.1 copy.75
  10.2 0.7 multiply_add_fusion
  10.9 0.5 fusion
  11.4 1.0 convolution_convert_fusion.1
  12.4 0.2 copy.76
  12.6 21.3 %all_to_all.15 = bf16[32,2,16,160]{3,2,1,0:T(8,128)(2,1)S(1)} all-to-all(bf16[32,2,16,160]{3,2,1,0:T(8,128)(2,1)S(1)} %bitcast.59), channel_id=1, replica_groups=mesh['row'=32,'col'=16] {'row'}, dimensions={0} | all-to-all | bytes 655360 | tf_op jit(solution)/shard_map/all_to_all | solution.py:54
  33.9 2.3 copy.77
  36.2 0.0 all-gather.2.cloned.1.call-update
  36.2 231.6 %all-gather.2.cloned.1.call-done = bf16[32,2,16,2560]{0,2,1,3:T(8,128)(2,1)} async-done(((bf16[32,2,16,160]{0,2,1,3:T(8,128)(2,1)}), bf16[32,2,16,2560]{0,2,1,3:T(8,128)(2,1)}) %all-gather.2.cloned.1.call-update) | async-done | bytes 5242896 | tf_op jit(solution)/shard_map/all_gather | solution.py:55
  267.8 10.4 %constant_dynamic-slice_fusion = bf16[32,1,16,2560]{0,2,1,3:T(8,128)(2,1)} fusion(bf16[32,2,16,2560]{0,2,1,3:T(8,128)(2,1)} %all-gather.2.cloned.1.call-done, s32[]{:T(128)S(6)} %select_n.19), kind=kLoop, calls=%fused_computation.47 | loop fusion | bytes 5242884 | tf_op jit(solution)/shard_map/jit(dynamic_index_in_dim)/dynamic_slice | solution.py:57
  278.2 0.0 copy-start.6
  278.2 13.0 %copy.86 = bf16[32,1,16,2560]{3,2,0,1:T(8,128)(2,1)} copy(bf16[32,1,16,2560]{0,2,1,3:T(8,128)(2,1)} %constant_dynamic-slice_fusion) | data formatting | bytes 5242880
  291.2 0.0 copy-start.7
  291.2 0.0 copy-done.6
  291.2 2.8 fusion.9
  294.0 0.0 copy-done
  294.0 0.0 copy-done.7
  294.1 5.2 %convolution_convert_fusion = bf16[512,2560]{1,0:T(8,128)(2,1)} fusion(bf16[512,2560]{1,0:T(8,128)(2,1)} %bitcast.58, bf16[1,192,2560]{2,1,0:T(8,128)(2,1)S(1)} %copy-done, bf16[1,192,2560]{2,1,0:T(8,128)(2,1)S(1)} %copy-done.7, f32[512,192]{0,1:T(8,128)S(1)} %fusion.9), kind=kOutput, calls=%fused_computation.1 | convolution fusion | flops 1008533504 | bytes 7602176 | tf_op jit(solution)/shard_map/dot_general | solution.py:63
  299.2 4.4 copy.79
  303.6 0.0 copy-start.5
  303.6 0.0 copy-start.2
  303.6 0.0 copy-start.8
  303.6 0.0 copy-start.9
  303.6 8.8 %all-to-all-start.1 = ((bf16[512,16,160]{0,2,1:T(8,128)(2,1)}), bf16[512,16,160]{0,2,1:T(8,128)(2,1)}, u32[]{:S(2)}, u32[]{:S(2)}) async-start(bf16[512,16,160]{0,2,1:T(8,128)(2,1)} %bitcast.55), calls=%async_computation.1 | async-start | bytes 5242880 | tf_op jit(solution)/shard_map/all_to_all | solution.py:67
  312.4 0.0 copy-done.5
  312.4 0.1 copy.82
  312.5 0.1 reduce.2
  312.6 0.0 copy-done.2
  312.7 25.6 %all_gather.10 = bf16[64,16,160]{2,1,0:T(8,128)(2,1)S(1)} all-gather(bf16[2,16,160]{2,1,0:T(8,128)(2,1)S(1)} %copy-done.2), channel_id=1, replica_groups=mesh['row'=32,'col'=16] {'row'}, dimensions={0}, use_global_device_ids=true | all-gather | bytes 337920 | tf_op jit(solution)/shard_map/all_gather | solution.py:77
  338.2 0.0 copy-done.8
  338.2 0.1 convert_reduce_fusion.1
  338.3 0.0 copy-done.9
  338.3 0.1 select_reduce_fusion.1
  338.4 88.4 %all-to-all-done.1 = bf16[512,16,160]{0,2,1:T(8,128)(2,1)} async-done(((bf16[512,16,160]{0,2,1:T(8,128)(2,1)}), bf16[512,16,160]{0,2,1:T(8,128)(2,1)}, u32[]{:S(2)}, u32[]{:S(2)}) %all-to-all-start.1) | async-done | bytes 2621472 | tf_op jit(solution)/shard_map/all_to_all | solution.py:67
  426.8 2.2 convert_reduce_fusion
  428.9 0.0 copy-start.1
  429.0 0.0 copy-start.3
  429.0 0.0 copy-start.4
  429.0 1.3 copy.85
  430.3 11.3 %all-to-all-start.2 = ((f32[32,2,16,160]{3,1,2,0:T(2,128)}), f32[32,2,16,160]{3,1,2,0:T(2,128)S(1)}, u32[]{:S(2)}, u32[]{:S(2)}) async-start(f32[32,2,16,160]{3,1,2,0:T(2,128)} %bitcast.10), calls=%async_computation.2 | async-start | bytes 2097152 | tf_op jit(solution)/shard_map/all_to_all | solution.py:72
  441.6 0.0 copy-done.1
  441.6 0.3 fusion.2
  441.9 22.3 %psum.7 = bf16[128,16]{0,1:T(8,128)(2,1)S(1)} all-reduce(f32[128,16]{0,1:T(8,128)S(1)} %fusion.2), channel_id=1, replica_groups=mesh['row'=32,'col'=16] {'col'}, use_global_device_ids=true, to_apply=%region_10.11 | all-reduce | flops 2048 | bytes 12288 | tf_op jit(solution)/shard_map/psum | solution.py:103
  464.2 0.0 copy-done.3
  464.2 31.2 %all_gather.11 = bf16[64,16,160]{2,1,0:T(8,128)(2,1)S(1)} all-gather(bf16[2,16,160]{2,1,0:T(8,128)(2,1)S(1)} %copy-done.3), channel_id=1, replica_groups=mesh['row'=32,'col'=16] {'row'}, dimensions={0}, use_global_device_ids=true | all-gather | bytes 337920 | tf_op jit(solution)/shard_map/all_gather | solution.py:78
  495.4 0.0 copy-done.4
  495.5 0.4 select_reduce_fusion
  495.9 0.0 all-to-all-done.2
  495.9 0.1 copy.81
  496.0 1.8 fusion.29
  497.8 1.0 fusion.5
  (5 shorter events, 0.1 us)
Async XLA Ops:
  6.5 287.5 %copy-start = (bf16[1,192,2560]{2,1,0:T(8,128)(2,1)S(1)}, bf16[1,192,2560]{2,1,0:T(8,128)(2,1)}, u32[]{:S(2)}) copy-start(bf16[1,192,2560]{2,1,0:T(8,128)(2,1)} %param.14) | copy-start | bytes 2949124
  6.5 261.2 %all-gather.2.cloned.1.call-start = ((), (), s32[]{:S(2)}) async-start(), calls=%async_computation.3 | async-start | bytes 22282240 | tf_op jit(solution)/shard_map/all_gather | solution.py:55
  278.2 13.1 %copy-start.6 = (bf16[1,192,2560]{2,1,0:T(8,128)(2,1)S(1)}, bf16[1,192,2560]{2,1,0:T(8,128)(2,1)}, u32[]{:S(2)}) copy-start(bf16[1,192,2560]{2,1,0:T(8,128)(2,1)} %param.12) | copy-start | bytes 2949124
  291.2 2.8 copy-start.7
  303.6 8.8 %copy-start.5 = (s32[16]{0:T(128)S(1)}, s32[16]{0:T(128)}, u32[]{:S(2)}) copy-start(s32[16]{0:T(128)} %param.19) | copy-start | bytes 196
  303.6 9.0 %copy-start.2 = (bf16[2,16,160]{2,1,0:T(8,128)(2,1)S(1)}, bf16[2,16,160]{2,1,0:T(8,128)(2,1)}, u32[]{:S(2)}) copy-start(bf16[2,16,160]{2,1,0:T(8,128)(2,1)} %param.15) | copy-start | bytes 30724
  303.6 34.6 %copy-start.8 = (s32[128]{0:T(128)S(1)}, s32[128]{0:T(128)}, u32[]{:S(2)}) copy-start(s32[128]{0:T(128)} %param.20) | copy-start | bytes 1540
  303.6 34.7 %copy-start.9 = (s32[16]{0:T(128)S(1)}, s32[16]{0:T(128)}, u32[]{:S(2)}) copy-start(s32[16]{0:T(128)} %param.21) | copy-start | bytes 196
  303.6 123.2 %all-to-all-start.1 = ((bf16[512,16,160]{0,2,1:T(8,128)(2,1)}), bf16[512,16,160]{0,2,1:T(8,128)(2,1)}, u32[]{:S(2)}, u32[]{:S(2)}) async-start(bf16[512,16,160]{0,2,1:T(8,128)(2,1)} %bitcast.55), calls=%async_computation.1 | async-start | bytes 5242880 | tf_op jit(solution)/shard_map/all_to_all | solution.py:67
  428.9 12.6 %copy-start.1 = (bf16[128,160]{0,1:T(8,128)(2,1)S(1)}, bf16[128,160]{0,1:T(8,128)(2,1)}, u32[]{:S(2)}) copy-start(bf16[128,160]{0,1:T(8,128)(2,1)} %param.11) | copy-start | bytes 122884
  429.0 35.3 %copy-start.3 = (bf16[2,16,160]{2,1,0:T(8,128)(2,1)S(1)}, bf16[2,16,160]{2,1,0:T(8,128)(2,1)}, u32[]{:S(2)}) copy-start(bf16[2,16,160]{2,1,0:T(8,128)(2,1)} %param.16) | copy-start | bytes 30724
  429.0 66.5 %copy-start.4 = (f32[128,6]{0,1:T(8,128)S(1)}, f32[128,6]{0,1:T(8,128)}, u32[]{:S(2)}) copy-start(f32[128,6]{0,1:T(8,128)} %param.18) | copy-start | bytes 9220
  430.3 65.6 %all-to-all-start.2 = ((f32[32,2,16,160]{3,1,2,0:T(2,128)}), f32[32,2,16,160]{3,1,2,0:T(2,128)S(1)}, u32[]{:S(2)}, u32[]{:S(2)}) async-start(f32[32,2,16,160]{3,1,2,0:T(2,128)} %bitcast.10), calls=%async_computation.2 | async-start | bytes 2097152 | tf_op jit(solution)/shard_map/all_to_all | solution.py:72
Sparse Core Ops, SparseCore 0:
  36.3 231.4 all-gather.1
where the time goes:
time: 507 us; the launch traced here: 506 us
  waiting for transfers between devices  320 us (63%)
  blocking collectives  100 us (20%)
  local copies, waits for them, and re-layouts  33.4 us (7%)
  starting transfers between devices  20 us (4%)
  between operations  13.6 us (3%)
  matrix products  12.1 us (2%)
  other arithmetic  6.11 us (1%)
    all_gather x1, waiting for transfers between devices, body(): piece = lax.all_gather(arrival_rows, 'col', axis=3, tiled=True)  232 us
    all_to_all x1, waiting for transfers between devices, body(): lax.all_to_all(pieces, 'col', split_axis=1, concat_axis=1, tiled=True)  88.4 us
    all_gather x1, blocking collectives, body(): lax.all_gather(adp_up, 'row', axis=0, tiled=True)  31.2 us
    all_gather x1, blocking collectives, body(): lax.all_gather(adp_down, 'row', axis=0, tiled=True)  25.6 us
    psum x1, blocking collectives, body(): low = lax.psum(partial_low, 'col').astype(jnp.bfloat16)  22.3 us
    all_to_all x1, blocking collectives, body(): lax.all_to_all(outgoing, 'row', split_axis=0, concat_axis=0, tiled=True)  21.3 us
    unnamed x23, local copies, waits for them, and re-layouts  15.3 us
    all_to_all x1, starting transfers between devices, body(): lax.all_to_all(summed, 'row', split_axis=0, concat_axis=0, tiled=True)  11.3 us
  transfers between devices with their start and end apart: 3, of which 2 were waited for; matrix products, arithmetic and copies ran while one was open for 0% of the time, Pallas kernels for 0%

commit v1 on v0

v1 whole, which is shorter than its diff:
```python
import jax
import jax.numpy as jnp
from jax import lax
from jax.sharding import PartitionSpec as P

adapter_scale_factor = 2.0


def contract(left, right, left_dim, right_dim):
    return lax.dot_general(
        left, right, (((left_dim,), (right_dim,)), ((), ())), preferred_element_type=jnp.float32
    )


def split_pair(value):
    high = lax.reduce_precision(value, 8, 7)
    return high.astype(jnp.bfloat16), (value - high).astype(jnp.bfloat16)


def spread(value, axis_name):
    count = lax.axis_size(axis_name)
    copies = jnp.broadcast_to(value[None], (count,) + value.shape)
    return lax.all_to_all(copies, axis_name, split_axis=0, concat_axis=0, tiled=True)


def body(
    tokens,
    w_gate,
    w_up,
    w_down,
    adp_down,
    adp_up,
    expert_ids,
    gate_vals,
    lengths,
    perm,
    req_adapter,
):
    count_tok = tokens.shape[0]
    share = tokens.shape[1]
    rows_count = lax.axis_size("row")
    cols_count = lax.axis_size("col")
    experts = 2 * rows_count
    parts = cols_count // 2
    which = lax.axis_index("col") // parts
    topk = expert_ids.shape[1]
    capacity = max(2, (4 * count_tok * topk + 3 * experts - 1) // (3 * experts))
    slots = rows_count * capacity
    features = cols_count * share
    rank = adp_down.shape[1]
    own_adapters = adp_down.shape[0]
    adapters = own_adapters * rows_count

    tokens_t = tokens.T
    full_t = spread(tokens_t, "col").reshape(features, count_tok)

    flat_ids = expert_ids.reshape(-1)
    onehot = (flat_ids[:, None] == jnp.arange(experts, dtype=jnp.int32)[None, :]).astype(jnp.int32)
    slot = jnp.sum(onehot * jnp.cumsum(onehot, axis=0), axis=1) - 1
    place = jnp.where(flat_ids % 2 == which, (flat_ids // 2) * capacity + slot, slots)
    place = place.reshape(count_tok, topk).T
    targets = jnp.arange(slots, dtype=jnp.int32)
    hit = targets[:, None, None] == place[None, :, :]
    dispatch = jnp.any(hit, axis=1).astype(jnp.bfloat16)
    combine = jnp.sum(jnp.where(hit, gate_vals.T[None, :, :], jnp.float32(0.0)), axis=1)
    combine = jnp.concatenate(split_pair(combine), axis=1)

    outgoing = contract(dispatch, full_t, 1, 1).astype(jnp.bfloat16)
    outgoing = outgoing.reshape(rows_count, capacity, features)
    mine = lax.all_to_all(outgoing, "row", split_axis=0, concat_axis=0, tiled=True)
    mine = mine.reshape(slots, features)
    gate = contract(mine, w_gate[0], 1, 1)
    upper = contract(mine, w_up[0], 1, 1)
    hidden = (jax.nn.silu(gate) * upper).astype(jnp.bfloat16)
    partial_out = contract(hidden, w_down[0], 1, 0).astype(jnp.bfloat16)
    partial_out = partial_out.reshape(rows_count, capacity, features)
    returned = lax.all_to_all(partial_out, "row", split_axis=0, concat_axis=0, tiled=True)
    returned = returned.reshape(slots, features)
    routed_t = contract(returned, combine, 0, 0)
    routed_t = (routed_t[:, :count_tok] + routed_t[:, count_tok:]).astype(jnp.bfloat16)

    maps = jnp.concatenate(
        [adp_down.reshape(own_adapters * rank, share), adp_up.reshape(own_adapters * rank, share)]
    )
    maps = spread(maps, "row").reshape(rows_count, 2, own_adapters * rank, share)
    down_all = maps[:, 0].reshape(adapters * rank, share)
    up_all = maps[:, 1].reshape(adapters * rank, share)
    nreq = lengths.shape[0]
    ends = jnp.cumsum(lengths)
    request = jnp.sum((perm[:, None] >= ends[None, :]).astype(jnp.int32), axis=1)
    adapter = jnp.sum(
        jnp.where(
            request[:, None] == jnp.arange(nreq, dtype=jnp.int32)[None, :], req_adapter[None, :], 0
        ),
        axis=1,
    )
    chosen = jnp.arange(adapters, dtype=jnp.int32)[:, None, None] == adapter[None, None, :]
    projected = contract(down_all, tokens_t, 1, 0).reshape(adapters, rank, count_tok)
    partial_low = jnp.sum(jnp.where(chosen, projected, jnp.float32(0.0)), axis=0)
    low_high, low_rest = split_pair(partial_low)

    extra = jnp.concatenate([low_high, low_rest])
    extra = jnp.broadcast_to(extra[None], (cols_count,) + extra.shape)
    sent = jnp.concatenate([routed_t.reshape(cols_count, share, count_tok), extra], axis=1)
    arrived = lax.all_to_all(sent, "col", split_axis=0, concat_axis=0, tiled=True)
    total = jnp.sum(arrived.astype(jnp.float32), axis=0)
    low = (total[share : share + rank] + total[share + rank :]).astype(jnp.bfloat16)
    expanded = jnp.where(chosen, low[None], jnp.bfloat16(0.0)).reshape(adapters * rank, count_tok)
    delta_t = contract(up_all, expanded, 0, 0)
    return (total[:share] + adapter_scale_factor * delta_t).T.astype(jnp.bfloat16)


def solution(mesh):
    in_specs = (
        P("row", "col"),
        P(("row", "col"), None, None),
        P(("row", "col"), None, None),
        P(("row", "col"), None, None),
        P("row", None, "col"),
        P("row", None, "col"),
        P("row", None),
        P("row", None),
        P(),
        P("row"),
        P(),
    )
    out_specs = P("row", "col")
    return jax.shard_map(body, mesh=mesh, in_specs=in_specs, out_specs=out_specs, check_vma=False)
```

time: 507 us -> 209 us (0.41)
  the two profiles are of different devices: /device:TPU:1 before, /device:TPU:64 now
where the time goes in v1:
time: 209 us; the launch traced here: 208 us
  waiting for transfers between devices  106 us (51%)
  blocking collectives  49 us (23%)
  starting transfers between devices  31.2 us (15%)
  matrix products  14.4 us (7%)
  local copies, waits for them, and re-layouts  4.65 us (2%)
  other arithmetic  3.24 us (2%)
    all_to_all x1, blocking collectives, body(): lax.all_to_all(sent, 'col', split_axis=0, concat_axis=0, tiled=True)  49 us
    all_to_all x2, waiting for transfers between devices, spread(): lax.all_to_all(copies, axis_name, split_axis=0, concat_axis=0, tiled=True)  37.6 us
    all_to_all x1, waiting for transfers between devices, body(): lax.all_to_all(outgoing, 'row', split_axis=0, concat_axis=0, tiled=True)  34.6 us
    all_to_all x1, waiting for transfers between devices, body(): lax.all_to_all(partial_out, 'row', split_axis=0, concat_axis=0, tiled=True)  33.5 us
    all_to_all x2, starting transfers between devices, spread(): lax.all_to_all(copies, axis_name, split_axis=0, concat_axis=0, tiled=True)  18.7 us
    dot_general x6, matrix products, contract(): lax.dot_general(left, right, (((left_dim,), (right_dim,)), ((), ())), pre...  14.4 us
    all_to_all x1, starting transfers between devices, body(): lax.all_to_all(outgoing, 'row', split_axis=0, concat_axis=0, tiled=True)  7.56 us
    all_to_all x1, starting transfers between devices, body(): lax.all_to_all(partial_out, 'row', split_axis=0, concat_axis=0, tiled=True)  4.95 us
  transfers between devices with their start and end apart: 4, of which 4 were waited for; matrix products, arithmetic and copies ran while one was open for 6% of the time, Pallas kernels for 0%

profile of v1, /device:TPU:64, one launch (start us, length us, event | category | flops | bytes accessed | tf_op | source)
XLA Modules:
  0.0 208.5 jit_solution(7196127984030278578)
XLA Ops:
  0.0 0.0 copy-start
  0.0 1.8 broadcast_in_dim.89
  1.8 14.8 %all-to-all-start = ((bf16[16,160,128]{2,1,0:T(8,128)(2,1)}), bf16[16,160,128]{2,1,0:T(8,128)(2,1)S(1)}, u32[]{:S(2)}, u32[]{:S(2)}) async-start(bf16[16,160,128]{2,1,0:T(8,128)(2,1)} %broadcast_in_dim.89), calls=%async_computation | async-start | bytes 1310720 | tf_op jit(solution)/shard_map/all_to_all | solution.py:23
  16.5 0.8 copy.22
  17.3 0.1 eq.85
  17.5 0.1 eq.81
  17.6 1.8 reduce-window.18
  19.4 0.3 slice_reduce_fusion
  19.7 0.1 fusion.23
  19.9 0.1 sub.25
  20.1 0.1 fusion.30
  20.1 0.1 copy.29
  20.2 0.2 fusion
  20.4 29.0 %all-to-all-done = bf16[16,160,128]{2,1,0:T(8,128)(2,1)S(1)} async-done(((bf16[16,160,128]{2,1,0:T(8,128)(2,1)}), bf16[16,160,128]{2,1,0:T(8,128)(2,1)S(1)}, u32[]{:S(2)}, u32[]{:S(2)}) %all-to-all-start) | async-done | bytes 655392 | tf_op jit(solution)/shard_map/all_to_all | solution.py:23
  49.4 2.4 %convolution_convert_fusion.1 = bf16[512,2560]{1,0:T(8,128)(2,1)} fusion(pred[512,128]{1,0:T(8,128)(4,1)S(1)} %fusion, bf16[2560,128]{1,0:T(8,128)(2,1)S(1)} %bitcast.58), kind=kOutput, calls=%fused_computation.1 | convolution fusion | flops 336855040 | bytes 3342336 | tf_op jit(solution)/shard_map/dot_general | solution.py:10
  51.8 0.0 copy-start.2
  51.8 0.0 copy-start.3
  51.8 7.6 %all-to-all-start.1 = ((bf16[32,16,2560]{2,1,0:T(8,128)(2,1)}), bf16[32,16,2560]{2,1,0:T(8,128)(2,1)}, u32[]{:S(2)}, u32[]{:S(2)}) async-start(bf16[32,16,2560]{2,1,0:T(8,128)(2,1)} %bitcast.56), calls=%async_computation.1 | async-start | bytes 5242880 | tf_op jit(solution)/shard_map/all_to_all | solution.py:70
  59.4 0.0 copy-start.6
  59.4 0.0 copy-done.2
  59.4 0.0 copy-done.3
  59.4 34.6 %all-to-all-done.1 = bf16[32,16,2560]{2,1,0:T(8,128)(2,1)} async-done(((bf16[32,16,2560]{2,1,0:T(8,128)(2,1)}), bf16[32,16,2560]{2,1,0:T(8,128)(2,1)}, u32[]{:S(2)}, u32[]{:S(2)}) %all-to-all-start.1) | async-done | bytes 2621472 | tf_op jit(solution)/shard_map/all_to_all | solution.py:70
  94.0 1.1 broadcast_in_dim.95
  95.2 3.9 %all-to-all-start.3 = ((bf16[32,64,160]{2,1,0:T(8,128)(2,1)}), bf16[32,64,160]{2,1,0:T(8,128)(2,1)S(1)}, u32[]{:S(2)}, u32[]{:S(2)}) async-start(bf16[32,64,160]{2,1,0:T(8,128)(2,1)} %broadcast_in_dim.95), calls=%async_computation.3 | async-start | bytes 2097152 | tf_op jit(solution)/shard_map/all_to_all | solution.py:23
  99.1 0.0 copy-done.6
  99.1 2.7 %fusion.10 = f32[512,192]{0,1:T(8,128)S(1)} fusion(bf16[512,2560]{1,0:T(8,128)(2,1)} %bitcast.5, bf16[1,192,2560]{2,1,0:T(8,128)(2,1)S(1)} %copy-done.6), kind=kOutput, calls=%fused_computation.18 | convolution fusion | flops 503316480 | bytes 3997696 | tf_op jit(solution)/shard_map/dot_general | solution.py:10
  101.9 0.0 copy-done
  101.9 5.4 %convolution_convert_fusion = bf16[512,2560]{1,0:T(8,128)(2,1)} fusion(bf16[512,2560]{1,0:T(8,128)(2,1)} %bitcast.5, bf16[1,192,2560]{2,1,0:T(8,128)(2,1)S(1)} %copy-done, bf16[1,192,2560]{2,1,0:T(8,128)(2,1)} %param.13, f32[512,192]{0,1:T(8,128)S(1)} %fusion.10), kind=kOutput, calls=%fused_computation | convolution fusion | flops 1008533504 | bytes 7602176 | tf_op jit(solution)/shard_map/dot_general | solution.py:10
  107.3 8.6 %all-to-all-done.3 = bf16[32,64,160]{2,1,0:T(8,128)(2,1)S(1)} async-done(((bf16[32,64,160]{2,1,0:T(8,128)(2,1)}), bf16[32,64,160]{2,1,0:T(8,128)(2,1)S(1)}, u32[]{:S(2)}, u32[]{:S(2)}) %all-to-all-start.3) | async-done | bytes 655392 | tf_op jit(solution)/shard_map/all_to_all | solution.py:23
  115.9 0.0 copy-start.5
  115.9 0.0 copy-start.7
  115.9 0.0 copy-start.8
  115.9 0.0 copy-start.4
  115.9 4.9 %all-to-all-start.2 = ((bf16[32,16,2560]{2,1,0:T(8,128)(2,1)}), bf16[32,16,2560]{2,1,0:T(8,128)(2,1)}, u32[]{:S(2)}, u32[]{:S(2)}) async-start(bf16[32,16,2560]{2,1,0:T(8,128)(2,1)} %bitcast.59), calls=%async_computation.2 | async-start | bytes 5242880 | tf_op jit(solution)/shard_map/all_to_all | solution.py:77
  120.9 0.0 copy-start.1
  120.9 0.0 copy-done.5
  120.9 0.1 copy.30
  121.0 0.1 reduce.1
  121.1 0.0 copy-done.7
  121.1 0.1 convert_reduce_fusion.1
  121.2 0.0 copy-done.8
  121.2 0.1 select_reduce_fusion.1
  121.3 0.0 copy-done.4
  121.3 0.2 select_reduce_fusion
  121.6 0.1 fusion.38
  121.6 0.0 copy-done.1
  121.6 0.3 fusion.3
  122.0 33.5 %all-to-all-done.2 = bf16[32,16,2560]{2,1,0:T(8,128)(2,1)} async-done(((bf16[32,16,2560]{2,1,0:T(8,128)(2,1)}), bf16[32,16,2560]{2,1,0:T(8,128)(2,1)}, u32[]{:S(2)}, u32[]{:S(2)}) %all-to-all-start.2) | async-done | bytes 2621472 | tf_op jit(solution)/shard_map/all_to_all | solution.py:77
  155.5 2.6 %fusion.18 = f32[2560,256]{1,0:T(8,128)S(1)} fusion(bf16[512,2560]{1,0:T(8,128)(2,1)} %bitcast.10, bf16[512,128]{1,0:T(8,128)(2,1)S(1)} %get-tuple-element.8, bf16[512,128]{1,0:T(8,128)(2,1)S(1)} %get-tuple-element.7), kind=kOutput, calls=%fused_computation.29 | convolution fusion | flops 671612928 | bytes 5505024 | tf_op jit(solution)/shard_map/dot_general | solution.py:10
  158.1 0.1 fusion.1
  158.3 0.1 pad_maximum_fusion
  158.3 49.0 %all_to_all.25 = bf16[16,192,128]{2,1,0:T(8,128)(2,1)S(1)} all-to-all(bf16[16,192,128]{2,1,0:T(8,128)(2,1)S(1)} %pad_maximum_fusion), channel_id=1, replica_groups=mesh['row'=32,'col'=16] {'col'}, dimensions={0} | all-to-all | bytes 1572864 | tf_op jit(solution)/shard_map/all_to_all | solution.py:105
  207.4 0.1 convert_reduce_fusion
  207.5 0.1 broadcast_select_fusion
  207.6 0.9 fusion.6
  (11 shorter events, 0.2 us)
Async XLA Ops:
  0.0 101.9 %copy-start = (bf16[1,192,2560]{2,1,0:T(8,128)(2,1)S(1)}, bf16[1,192,2560]{2,1,0:T(8,128)(2,1)}, u32[]{:S(2)}) copy-start(bf16[1,192,2560]{2,1,0:T(8,128)(2,1)} %param.14) | copy-start | bytes 2949124
  1.8 47.7 %all-to-all-start = ((bf16[16,160,128]{2,1,0:T(8,128)(2,1)}), bf16[16,160,128]{2,1,0:T(8,128)(2,1)S(1)}, u32[]{:S(2)}, u32[]{:S(2)}) async-start(bf16[16,160,128]{2,1,0:T(8,128)(2,1)} %broadcast_in_dim.89), calls=%async_computation | async-start | bytes 1310720 | tf_op jit(solution)/shard_map/all_to_all | solution.py:23
  51.8 7.6 %copy-start.2 = (bf16[2,16,160]{2,1,0:T(8,128)(2,1)S(1)}, bf16[2,16,160]{2,1,0:T(8,128)(2,1)}, u32[]{:S(2)}) copy-start(bf16[2,16,160]{2,1,0:T(8,128)(2,1)} %param.16) | copy-start | bytes 30724
  51.8 7.6 %copy-start.3 = (bf16[2,16,160]{2,1,0:T(8,128)(2,1)S(1)}, bf16[2,16,160]{2,1,0:T(8,128)(2,1)}, u32[]{:S(2)}) copy-start(bf16[2,16,160]{2,1,0:T(8,128)(2,1)} %param.15) | copy-start | bytes 30724
  51.8 42.2 %all-to-all-start.1 = ((bf16[32,16,2560]{2,1,0:T(8,128)(2,1)}), bf16[32,16,2560]{2,1,0:T(8,128)(2,1)}, u32[]{:S(2)}, u32[]{:S(2)}) async-start(bf16[32,16,2560]{2,1,0:T(8,128)(2,1)} %bitcast.56), calls=%async_computation.1 | async-start | bytes 5242880 | tf_op jit(solution)/shard_map/all_to_all | solution.py:70
  59.4 39.7 %copy-start.6 = (bf16[1,192,2560]{2,1,0:T(8,128)(2,1)S(1)}, bf16[1,192,2560]{2,1,0:T(8,128)(2,1)}, u32[]{:S(2)}) copy-start(bf16[1,192,2560]{2,1,0:T(8,128)(2,1)} %param.12) | copy-start | bytes 2949124
  95.2 20.7 %all-to-all-start.3 = ((bf16[32,64,160]{2,1,0:T(8,128)(2,1)}), bf16[32,64,160]{2,1,0:T(8,128)(2,1)S(1)}, u32[]{:S(2)}, u32[]{:S(2)}) async-start(bf16[32,64,160]{2,1,0:T(8,128)(2,1)} %broadcast_in_dim.95), calls=%async_computation.3 | async-start | bytes 2097152 | tf_op jit(solution)/shard_map/all_to_all | solution.py:23
  115.9 5.0 %copy-start.5 = (s32[16]{0:T(128)S(1)}, s32[16]{0:T(128)}, u32[]{:S(2)}) copy-start(s32[16]{0:T(128)} %param.19) | copy-start | bytes 196
  115.9 5.2 %copy-start.7 = (s32[128]{0:T(128)S(1)}, s32[128]{0:T(128)}, u32[]{:S(2)}) copy-start(s32[128]{0:T(128)} %param.20) | copy-start | bytes 1540
  115.9 5.3 %copy-start.8 = (s32[16]{0:T(128)S(1)}, s32[16]{0:T(128)}, u32[]{:S(2)}) copy-start(s32[16]{0:T(128)} %param.21) | copy-start | bytes 196
  115.9 5.4 %copy-start.4 = (f32[128,6]{0,1:T(8,128)S(1)}, f32[128,6]{0,1:T(8,128)}, u32[]{:S(2)}) copy-start(f32[128,6]{0,1:T(8,128)} %param.18) | copy-start | bytes 9220
  115.9 39.6 %all-to-all-start.2 = ((bf16[32,16,2560]{2,1,0:T(8,128)(2,1)}), bf16[32,16,2560]{2,1,0:T(8,128)(2,1)}, u32[]{:S(2)}, u32[]{:S(2)}) async-start(bf16[32,16,2560]{2,1,0:T(8,128)(2,1)} %bitcast.59), calls=%async_computation.2 | async-start | bytes 5242880 | tf_op jit(solution)/shard_map/all_to_all | solution.py:77
  120.9 0.8 copy-start.1

commit v2 on v1

--- a/solution.py
+++ b/solution.py
@@ -1,7 +1,14 @@
+import functools
+
 import jax
 import jax.numpy as jnp
 from jax import lax
+from jax.experimental import pallas as pl
+from jax.experimental.pallas import tpu as pltpu
 from jax.sharding import PartitionSpec as P
+
+MESH = pl.DeviceIdType.MESH
+VMEM = pl.BlockSpec(memory_space=pltpu.VMEM)
 
 adapter_scale_factor = 2.0
 
@@ -17,10 +24,190 @@
     return high.astype(jnp.bfloat16), (value - high).astype(jnp.bfloat16)
 
 
-def spread(value, axis_name):
-    count = lax.axis_size(axis_name)
-    copies = jnp.broadcast_to(value[None], (count,) + value.shape)
-    return lax.all_to_all(copies, axis_name, split_axis=0, concat_axis=0, tiled=True)
+def remote(src, dst, send_sem, recv_sem, axis_name, peer):
+    return pltpu.make_async_remote_copy(
+        src_ref=src,
+        dst_ref=dst,
+        send_sem=send_sem,
+        recv_sem=recv_sem,
+        device_id={axis_name: peer},
+        device_id_type=MESH,
+    )
+
+
+def gather_kernel(
+    rows, cols, tok_ref, maps_ref, full_ref, all_ref, own_sem, ring_send, ring_recv, row_send, row_recv
+):
+    me_r, me_c = lax.axis_index("row"), lax.axis_index("col")
+    sides = (lax.rem(me_c + 1, cols), lax.rem(me_c + cols - 1, cols))
+    hops = (cols // 2, cols - 1 - cols // 2)
+
+    barrier = pltpu.get_barrier_semaphore()
+    for side in sides:
+        pl.semaphore_signal(barrier, inc=1, device_id={"col": side}, device_id_type=MESH)
+
+    def greet(away, carry):
+        peer = lax.rem(me_r + away, rows)
+        pl.semaphore_signal(barrier, inc=1, device_id={"row": peer}, device_id_type=MESH)
+        return carry
+
+    lax.fori_loop(1, rows, greet, 0)
+    pl.semaphore_wait(barrier, rows + 1)
+
+    def shard(way, step):
+        return lax.rem(me_c + cols - step, cols) if way == 0 else lax.rem(me_c + step, cols)
+
+    def sending(way, step):
+        at = full_ref.at[shard(way, step)]
+        src = tok_ref if step == 0 else at
+        return remote(src, at, ring_send.at[way, step], ring_recv.at[way, step], "col", sides[way])
+
+    def arriving(way, step):
+        at = full_ref.at[shard(way, step + 1)]
+        return remote(at, at, ring_send.at[way, step], ring_recv.at[way, step], "col", sides[way])
+
+    def row_copy(away, owner):
+        at = all_ref.at[owner]
+        peer = lax.rem(me_r + away, rows)
+        return remote(maps_ref, at, row_send.at[away], row_recv.at[away], "row", peer)
+
+    for way in range(2):
+        sending(way, 0).start()
+
+    def row_start(away, carry):
+        row_copy(away, me_r).start()
+        return carry
+
+    lax.fori_loop(1, rows, row_start, 0)
+    own = (
+        pltpu.make_async_copy(tok_ref, full_ref.at[me_c], own_sem.at[0]),
+        pltpu.make_async_copy(maps_ref, all_ref.at[me_r], own_sem.at[1]),
+    )
+    for copy in own:
+        copy.start()
+    for step in range(max(hops)):
+        for way in range(2):
+            if step < hops[way]:
+                arriving(way, step).wait_recv()
+                if step + 1 < hops[way]:
+                    sending(way, step + 1).start()
+    for copy in own:
+        copy.wait()
+    for way in range(2):
+        for step in range(hops[way]):
+            sending(way, step).wait_send()
+
+    def row_end(away, carry):
+        copy = row_copy(away, lax.rem(me_r + rows - away, rows))
+        copy.wait_recv()
+        copy.wait_send()
+        return carry
+
+    lax.fori_loop(1, rows, row_end, 0)
+
+
+def gather(tokens_t, maps):
+    rows, cols = lax.axis_size("row"), lax.axis_size("col")
+    return pl.pallas_call(
+        functools.partial(gather_kernel, rows, cols),
+        out_shape=(
+            jax.ShapeDtypeStruct((cols,) + tokens_t.shape, tokens_t.dtype),
+            jax.ShapeDtypeStruct((rows,) + maps.shape, maps.dtype),
+        ),
+        in_specs=[VMEM] * 2,
+        out_specs=(VMEM, VMEM),
+        scratch_shapes=[
+            pltpu.SemaphoreType.DMA((2,)),
+            pltpu.SemaphoreType.DMA((2, cols)),
+            pltpu.SemaphoreType.DMA((2, cols)),
+            pltpu.SemaphoreType.DMA((rows,)),
+            pltpu.SemaphoreType.DMA((rows,)),
+        ],
+        compiler_params=pltpu.CompilerParams(collective_id=0, has_side_effects=True),
+    )(tokens_t, maps)
+
+
+def sum_kernel(
+    cols, part_ref, low_ref, total_ref, low_total_ref,
+    out_part, in_part, out_low, in_low, send_sem, recv_sem, low_send_sem, low_recv_sem,
+):
+    me = lax.axis_index("col")
+    sides = (lax.rem(me + 1, cols), lax.rem(me + cols - 1, cols))
+    half = cols // 2
+    hops = (half, cols - 1 - half)
+
+    barrier = pltpu.get_barrier_semaphore()
+    for side in sides:
+        pl.semaphore_signal(barrier, inc=1, device_id={"col": side}, device_id_type=MESH)
+    pl.semaphore_wait(barrier, 2)
+
+    def copies(way, step):
+        return (
+            remote(
+                out_part.at[way, step], in_part.at[way, step],
+                send_sem.at[way, step], recv_sem.at[way, step], "col", sides[way],
+            ),
+            remote(
+                out_low.at[way, step], in_low.at[way, step],
+                low_send_sem.at[way, step], low_recv_sem.at[way, step], "col", sides[way],
+            ),
+        )
+
+    for step in range(max(hops)):
+        for way in range(2):
+            if step >= hops[way]:
+                continue
+            if way == 0:
+                chunk = lax.rem(me + hops[0] - step, cols)
+            else:
+                chunk = lax.rem(me + cols - hops[1] + step, cols)
+            value, low = part_ref[chunk], low_ref[...]
+            if step > 0:
+                for copy in copies(way, step - 1):
+                    copy.wait_recv()
+                value = value + in_part[way, step - 1].astype(jnp.float32)
+                low = low + in_low[way, step - 1]
+            out_part[way, step] = value.astype(jnp.bfloat16)
+            out_low[way, step] = low
+            for copy in copies(way, step):
+                copy.start()
+    total, low = part_ref[me], low_ref[...]
+    for way in range(2):
+        last = hops[way] - 1
+        for copy in copies(way, last):
+            copy.wait_recv()
+        total = total + in_part[way, last].astype(jnp.float32)
+        low = low + in_low[way, last]
+    total_ref[...] = total
+    low_total_ref[...] = low
+    for way in range(2):
+        for step in range(hops[way]):
+            for copy in copies(way, step):
+                copy.wait_send()
+
+
+def sum_shares(parts, low):
+    cols, share, count_tok = parts.shape
+    hops = cols // 2
+    slots = (2, hops, share, count_tok)
+    low_slots = (2, hops) + low.shape
+    return pl.pallas_call(
+        functools.partial(sum_kernel, cols),
+        out_shape=(
+            jax.ShapeDtypeStruct((share, count_tok), jnp.float32),
+            jax.ShapeDtypeStruct(low.shape, jnp.float32),
+        ),
+        in_specs=[VMEM] * 2,
+        out_specs=(VMEM, VMEM),
+        scratch_shapes=[
+            pltpu.VMEM(slots, jnp.bfloat16),
+            pltpu.VMEM(slots, jnp.bfloat16),
+            pltpu.VMEM(low_slots, jnp.float32),
+            pltpu.VMEM(low_slots, jnp.float32),
+        ]
+        + [pltpu.SemaphoreType.DMA((2, hops))] * 4,
+        compiler_params=pltpu.CompilerParams(collective_id=1, has_side_effects=True),
+    )(parts, low)
 
 
 def body(
@@ -52,7 +239,11 @@
     adapters = own_adapters * rows_count
 
     tokens_t = tokens.T
-    full_t = spread(tokens_t, "col").reshape(features, count_tok)
+    maps = jnp.concatenate(
+        [adp_down.reshape(own_adapters * rank, share), adp_up.reshape(own_adapters * rank, share)]
+    )
+    full_t, maps = gather(tokens_t, maps)
+    full_t = full_t.reshape(features, count_tok)
 
     flat_ids = expert_ids.reshape(-1)
     onehot = (flat_ids[:, None] == jnp.arange(experts, dtype=jnp.int32)[None, :]).astype(jnp.int32)
@@ -77,12 +268,9 @@
     returned = lax.all_to_all(partial_out, "row", split_axis=0, concat_axis=0, tiled=True)
     returned = returned.reshape(slots, features)
     routed_t = contract(returned, combine, 0, 0)
-    routed_t = (routed_t[:, :count_tok] + routed_t[:, count_tok:]).astype(jnp.bfloat16)
-
-    maps = jnp.concatenate(
-        [adp_down.reshape(own_adapters * rank, share), adp_up.reshape(own_adapters * rank, share)]
-    )
-    maps = spread(maps, "row").reshape(rows_count, 2, own_adapters * rank, share)
+    routed_t = routed_t[:, :count_tok] + routed_t[:, count_tok:]
+
+    maps = maps.reshape(rows_count, 2, own_adapters * rank, share)
     down_all = maps[:, 0].reshape(adapters * rank, share)
     up_all = maps[:, 1].reshape(adapters * rank, share)
     nreq = lengths.shape[0]
@@ -97,17 +285,12 @@
     chosen = jnp.arange(adapters, dtype=jnp.int32)[:, None, None] == adapter[None, None, :]
     projected = contract(down_all, tokens_t, 1, 0).reshape(adapters, rank, count_tok)
     partial_low = jnp.sum(jnp.where(chosen, projected, jnp.float32(0.0)), axis=0)
-    low_high, low_rest = split_pair(partial_low)
-
-    extra = jnp.concatenate([low_high, low_rest])
-    extra = jnp.broadcast_to(extra[None], (cols_count,) + extra.shape)
-    sent = jnp.concatenate([routed_t.reshape(cols_count, share, count_tok), extra], axis=1)
-    arrived = lax.all_to_all(sent, "col", split_axis=0, concat_axis=0, tiled=True)
-    total = jnp.sum(arrived.astype(jnp.float32), axis=0)
-    low = (total[share : share + rank] + total[share + rank :]).astype(jnp.bfloat16)
+
+    total, low = sum_shares(routed_t.reshape(cols_count, share, count_tok), partial_low)
+    low = low.astype(jnp.bfloat16)
     expanded = jnp.where(chosen, low[None], jnp.bfloat16(0.0)).reshape(adapters * rank, count_tok)
     delta_t = contract(up_all, expanded, 0, 0)
-    return (total[:share] + adapter_scale_factor * delta_t).T.astype(jnp.bfloat16)
+    return (total + adapter_scale_factor * delta_t).T.astype(jnp.bfloat16)
 
 
 def solution(mesh):

time: 209 us -> 173 us (0.83)
  the two profiles are of different devices: /device:TPU:64 before, /device:TPU:8 now
where the time goes in v2:
time: 173 us; the launch traced here: 172 us
  Pallas kernels  73.9 us (43%)
  blocking collectives  37.5 us (22%)
  waiting for transfers between devices  31.7 us (18%)
  matrix products  13.4 us (8%)
  other arithmetic  6.16 us (4%)
  starting transfers between devices  5.82 us (3%)
  local copies, waits for them, and re-layouts  3.33 us (2%)
    pallas_call x1, Pallas kernels, gather(): pl.pallas_call(functools.partial(gather_kernel, rows, cols), out_shape=(j...  43 us
    all_to_all x1, blocking collectives, body(): lax.all_to_all(outgoing, 'row', split_axis=0, concat_axis=0, tiled=True)  37.5 us
    all_to_all x1, waiting for transfers between devices, body(): lax.all_to_all(partial_out, 'row', split_axis=0, concat_axis=0, tiled=True)  31.7 us
    pallas_call x1, Pallas kernels, sum_shares(): pl.pallas_call(functools.partial(sum_kernel, cols), out_shape=(jax.ShapeD...  30.8 us
    dot_general x6, matrix products, contract(): lax.dot_general(left, right, (((left_dim,), (right_dim,)), ((), ())), pre...  13.4 us
    all_to_all x1, starting transfers between devices, body(): lax.all_to_all(partial_out, 'row', split_axis=0, concat_axis=0, tiled=True)  5.82 us
  transfers between devices with their start and end apart: 1, of which 1 were waited for; matrix products, arithmetic and copies ran while one was open for 1% of the time, Pallas kernels for 0%

profile of v2, /device:TPU:8, one launch (start us, length us, event | category | flops | bytes accessed | tf_op | source)
XLA Modules:
  0.0 172.0 jit_solution(4358531858011204411)
XLA Ops:
  0.0 0.0 copy-start
  0.0 0.9 copy.22
  0.9 0.1 eq.85
  1.0 0.1 eq.81
  1.2 1.8 %reduce-window.18 = s32[64,6,128]{2,0,1:T(8,128)S(1)} reduce-window(s32[64,6,128]{2,0,1:T(8,128)S(1)} %fusion.24, s32[]{:T(128)} %constant.54.clone.1), window={size=1x1x128 pad=0_0x0_0x127_0}, to_apply=%region_0.1 | reduce-window | flops 6242304 | bytes 393220 | tf_op jit(solution)/shard_map/reduce-window
  3.0 0.3 slice_reduce_fusion
  3.3 0.1 fusion.22
  3.4 0.1 sub.22
  3.6 0.1 fusion.29
  3.7 0.1 copy.29
  3.7 0.2 fusion
  4.0 1.4 pad_maximum_fusion.maps_ref
  5.3 43.0 %shard_map.109 = (bf16[16,160,128]{2,1,0:T(8,128)(2,1)}, bf16[32,64,160]{2,1,0:T(8,128)(2,1)}) custom-call(bf16[160,128]{1,0:T(8,128)(2,1)} %bitcast.66, bf16[64,160]{1,0:T(8,128)(2,1)} %pad_maximum_fusion.maps_ref), custom_call_target="tpu_custom_call" | custom-call | tf_op jit(solution)/shard_map/pallas_call | solution.py:111
  48.4 1.9 %convolution_convert_fusion.1 = bf16[512,2560]{1,0:T(8,128)(2,1)S(1)} fusion(pred[512,128]{1,0:T(8,128)(4,1)S(1)} %fusion, bf16[2560,128]{1,0:T(8,128)(2,1)} %bitcast.64), kind=kOutput, calls=%fused_computation.1 | convolution fusion | flops 336855040 | bytes 3342336 | tf_op jit(solution)/shard_map/dot_general | solution.py:17
  50.3 0.0 copy-start.6
  50.3 37.5 %all_to_all.10 = bf16[32,16,2560]{2,1,0:T(8,128)(2,1)S(1)} all-to-all(bf16[32,16,2560]{2,1,0:T(8,128)(2,1)S(1)} %bitcast.56), channel_id=1, replica_groups=mesh['row'=32,'col'=16] {'row'}, dimensions={0} | all-to-all | bytes 5242880 | tf_op jit(solution)/shard_map/all_to_all | solution.py:261
  87.8 0.0 copy-start.1
  87.8 0.0 copy-start.7
  87.8 1.5 copy-done.1
  89.3 0.0 copy-done.6
  89.3 1.0 fusion.9
  90.3 0.0 copy-done
  90.3 0.0 copy-done.7
  90.4 5.1 %convolution_convert_fusion = bf16[512,2560]{1,0:T(8,128)(2,1)} fusion(bf16[512,2560]{1,0:T(8,128)(2,1)} %bitcast.60, bf16[1,192,2560]{2,1,0:T(8,128)(2,1)S(1)} %copy-done, bf16[1,192,2560]{2,1,0:T(8,128)(2,1)S(1)} %copy-done.7, f32[512,192]{0,1:T(8,128)S(1)} %fusion.9), kind=kOutput, calls=%fused_computation | convolution fusion | flops 1008533504 | bytes 7602176 | tf_op jit(solution)/shard_map/dot_general | solution.py:17
  95.5 0.0 copy-start.5
  95.5 0.0 copy-start.8
  95.5 0.0 copy-start.9
  95.5 0.0 copy-start.2
  95.5 0.0 copy-start.3
  95.5 5.8 %all-to-all-start.1 = ((bf16[32,16,2560]{2,1,0:T(8,128)(2,1)}), bf16[32,16,2560]{2,1,0:T(8,128)(2,1)}, u32[]{:S(2)}, u32[]{:S(2)}) async-start(bf16[32,16,2560]{2,1,0:T(8,128)(2,1)} %bitcast.58), calls=%async_computation.1 | async-start | bytes 5242880 | tf_op jit(solution)/shard_map/all_to_all | solution.py:268
  101.3 0.0 copy-start.4
  101.3 0.0 copy-done.5
  101.3 0.1 copy.30
  101.5 0.1 reduce.1
  101.6 0.0 copy-done.8
  101.6 0.1 convert_reduce_fusion
  101.7 0.0 copy-done.9
  101.7 0.1 select_reduce_fusion.1
  101.8 0.0 copy-done.2
  101.8 0.1 fusion.35
  101.9 0.0 copy-done.3
  101.9 0.9 fusion.2.low_ref
  102.8 0.0 copy-done.4
  102.8 0.2 select_reduce_fusion
  103.0 31.7 %all-to-all-done.1 = bf16[32,16,2560]{2,1,0:T(8,128)(2,1)} async-done(((bf16[32,16,2560]{2,1,0:T(8,128)(2,1)}), bf16[32,16,2560]{2,1,0:T(8,128)(2,1)}, u32[]{:S(2)}, u32[]{:S(2)}) %all-to-all-start.1) | async-done | bytes 2621472 | tf_op jit(solution)/shard_map/all_to_all | solution.py:268
  134.7 2.6 %fusion.17 = f32[2560,256]{1,0:T(8,128)S(1)} fusion(bf16[512,2560]{1,0:T(8,128)(2,1)} %bitcast.12, bf16[512,128]{1,0:T(8,128)(2,1)S(1)} %get-tuple-element.16, bf16[512,128]{1,0:T(8,128)(2,1)S(1)} %get-tuple-element.15), kind=kOutput, calls=%fused_computation.26 | convolution fusion | flops 671612928 | bytes 5505024 | tf_op jit(solution)/shard_map/dot_general | solution.py:17
  137.3 1.2 slice_add_fusion
  138.5 30.8 %shard_map.110 = (f32[160,128]{1,0:T(8,128)}, f32[16,128]{1,0:T(8,128)}) custom-call(f32[16,160,128]{2,1,0:T(8,128)} %bitcast.57, f32[16,128]{1,0:T(8,128)} %fusion.2.low_ref), custom_call_target="tpu_custom_call" | custom-call | tf_op jit(solution)/shard_map/pallas_call | solution.py:194
  169.4 0.7 convert_element_type.40
  170.1 0.1 broadcast_select_fusion
  170.1 1.8 %fusion.5 = bf16[128,160]{0,1:T(8,128)(2,1)} fusion(f32[160,128]{1,0:T(8,128)} %get-tuple-element.11, bf16[1024,160]{1,0:T(8,128)(2,1)S(1)} %bitcast.61, bf16[1024,128]{1,0:T(8,128)(2,1)S(1)} %bitcast.62), kind=kOutput, calls=%fused_computation.13 | convolution fusion | flops 42004480 | bytes 712704 | tf_op jit(solution)/shard_map/dot_general | solution.py:17
  (6 shorter events, 0.1 us)
Async XLA Ops:
  0.0 90.3 %copy-start = (bf16[1,192,2560]{2,1,0:T(8,128)(2,1)S(1)}, bf16[1,192,2560]{2,1,0:T(8,128)(2,1)}, u32[]{:S(2)}) copy-start(bf16[1,192,2560]{2,1,0:T(8,128)(2,1)} %param.14) | copy-start | bytes 2949124
  50.3 39.0 %copy-start.6 = (bf16[1,192,2560]{2,1,0:T(8,128)(2,1)S(1)}, bf16[1,192,2560]{2,1,0:T(8,128)(2,1)}, u32[]{:S(2)}) copy-start(bf16[1,192,2560]{2,1,0:T(8,128)(2,1)} %param.12) | copy-start | bytes 2949124
  87.8 1.5 copy-start.1
  87.8 2.5 %copy-start.7 = (bf16[1,192,2560]{2,1,0:T(8,128)(2,1)S(1)}, bf16[1,192,2560]{2,1,0:T(8,128)(2,1)}, u32[]{:S(2)}) copy-start(bf16[1,192,2560]{2,1,0:T(8,128)(2,1)} %param.13) | copy-start | bytes 2949124
  95.5 5.9 %copy-start.5 = (s32[16]{0:T(128)S(1)}, s32[16]{0:T(128)}, u32[]{:S(2)}) copy-start(s32[16]{0:T(128)} %param.19) | copy-start | bytes 196
  95.5 6.1 %copy-start.8 = (s32[128]{0:T(128)S(1)}, s32[128]{0:T(128)}, u32[]{:S(2)}) copy-start(s32[128]{0:T(128)} %param.20) | copy-start | bytes 1540
  95.5 6.2 %copy-start.9 = (s32[16]{0:T(128)S(1)}, s32[16]{0:T(128)}, u32[]{:S(2)}) copy-start(s32[16]{0:T(128)} %param.21) | copy-start | bytes 196
  95.5 6.3 %copy-start.2 = (bf16[32,64,160]{2,1,0:T(8,128)(2,1)S(1)}, bf16[32,64,160]{2,1,0:T(8,128)(2,1)}, u32[]{:S(2)}) copy-start(bf16[32,64,160]{2,1,0:T(8,128)(2,1)} %get-tuple-element.10) | copy-start | bytes 1966084
  95.5 6.4 %copy-start.3 = (bf16[128,160]{0,1:T(8,128)(2,1)S(1)}, bf16[128,160]{0,1:T(8,128)(2,1)}, u32[]{:S(2)}) copy-start(bf16[128,160]{0,1:T(8,128)(2,1)} %param.11) | copy-start | bytes 122884
  95.5 39.2 %all-to-all-start.1 = ((bf16[32,16,2560]{2,1,0:T(8,128)(2,1)}), bf16[32,16,2560]{2,1,0:T(8,128)(2,1)}, u32[]{:S(2)}, u32[]{:S(2)}) async-start(bf16[32,16,2560]{2,1,0:T(8,128)(2,1)} %bitcast.58), calls=%async_computation.1 | async-start | bytes 5242880 | tf_op jit(solution)/shard_map/all_to_all | solution.py:268
  101.3 1.5 copy-start.4

commit v3 on v2

--- a/solution.py
+++ b/solution.py
@@ -1,4 +1,5 @@
 import functools
+import math
 
 import jax
 import jax.numpy as jnp
@@ -35,6 +36,10 @@
     )
 
 
+def mixed(turn, rows):
+    return turn * (13 if math.gcd(13, rows) == 1 else 1) % rows
+
+
 def gather_kernel(
     rows, cols, tok_ref, maps_ref, full_ref, all_ref, own_sem, ring_send, ring_recv, row_send, row_recv
 ):
@@ -73,19 +78,16 @@
 
     for way in range(2):
         sending(way, 0).start()
-
-    def row_start(away, carry):
-        row_copy(away, me_r).start()
-        return carry
-
-    lax.fori_loop(1, rows, row_start, 0)
     own = (
         pltpu.make_async_copy(tok_ref, full_ref.at[me_c], own_sem.at[0]),
         pltpu.make_async_copy(maps_ref, all_ref.at[me_r], own_sem.at[1]),
     )
     for copy in own:
         copy.start()
+    batch = -(-(rows - 1) // max(hops))
     for step in range(max(hops)):
+        for turn in range(1 + step * batch, min(rows, 1 + (step + 1) * batch)):
+            row_copy(mixed(turn, rows), me_r).start()
         for way in range(2):
             if step < hops[way]:
                 arriving(way, step).wait_recv()
@@ -125,6 +127,103 @@
         ],
         compiler_params=pltpu.CompilerParams(collective_id=0, has_side_effects=True),
     )(tokens_t, maps)
+
+
+def expert_kernel(
+    rows, groups, pick_ref, full_ref, gate_ref, up_ref, down_ref, back_ref,
+    out_buf, in_buf, part_buf, out_send, out_recv, back_send, back_recv,
+):
+    me = lax.axis_index("row")
+    members = rows // groups
+    capacity, features = back_ref.shape[1:]
+    height = members * capacity
+    width = math.gcd(features, 512)
+
+    barrier = pltpu.get_barrier_semaphore()
+
+    def greet(away, carry):
+        peer = lax.rem(me + away, rows)
+        pl.semaphore_signal(barrier, inc=1, device_id={"row": peer}, device_id_type=MESH)
+        return carry
+
+    lax.fori_loop(1, rows, greet, 0)
+
+    def outward(turn):
+        peer = lax.rem(me + mixed(turn, rows), rows)
+        return remote(
+            out_buf.at[turn], in_buf.at[turn], out_send.at[turn], out_recv.at[turn], "row", peer
+        )
+
+    def homeward(turn):
+        peer = lax.rem(me + rows - mixed(turn, rows), rows)
+        return remote(
+            part_buf.at[turn], back_ref.at[turn], back_send.at[turn], back_recv.at[turn], "row", peer
+        )
+
+    def turns(group):
+        return [turn for turn in range(group * members, (group + 1) * members) if turn > 0]
+
+    for group in range(groups):
+        first = group * members
+        picks = pick_ref[group * height : (group + 1) * height, :]
+
+        def fill(tile, carry):
+            at = pl.multiple_of(tile * width, width)
+            block = contract(picks, full_ref[pl.ds(at, width), :], 1, 1).astype(jnp.bfloat16)
+            out_buf[first : first + members, :, pl.ds(at, width)] = block.reshape(
+                members, capacity, width
+            )
+            return carry
+
+        lax.fori_loop(0, features // width, fill, 0)
+        if group == 0:
+            pl.semaphore_wait(barrier, rows - 1)
+        for turn in turns(group):
+            outward(turn).start()
+    in_buf[0] = out_buf[0]
+
+    for group in range(groups):
+        first = group * members
+        for turn in turns(group):
+            outward(turn).wait_recv()
+        mine = in_buf[first : first + members].reshape(height, features)
+        gate = contract(mine, gate_ref[...], 1, 1)
+        upper = contract(mine, up_ref[...], 1, 1)
+        hidden = (jax.nn.silu(gate) * upper).astype(jnp.bfloat16)
+
+        def fill_part(tile, carry):
+            at = pl.multiple_of(tile * width, width)
+            block = contract(hidden, down_ref[:, pl.ds(at, width)], 1, 0).astype(jnp.bfloat16)
+            part_buf[first : first + members, :, pl.ds(at, width)] = block.reshape(
+                members, capacity, width
+            )
+            return carry
+
+        lax.fori_loop(0, features // width, fill_part, 0)
+        for turn in turns(group):
+            homeward(turn).start()
+    back_ref[0] = part_buf[0]
+    for turn in range(1, rows):
+        homeward(turn).wait_recv()
+    for turn in range(1, rows):
+        outward(turn).wait_send()
+        homeward(turn).wait_send()
+
+
+def run_experts(pick, full_t, gate, up, down):
+    rows = lax.axis_size("row")
+    features = full_t.shape[0]
+    blocks = (rows, pick.shape[0] // rows, features)
+    groups = math.gcd(rows, 4)
+    return pl.pallas_call(
+        functools.partial(expert_kernel, rows, groups),
+        out_shape=jax.ShapeDtypeStruct(blocks, jnp.bfloat16),
+        in_specs=[VMEM] * 5,
+        out_specs=VMEM,
+        scratch_shapes=[pltpu.VMEM(blocks, jnp.bfloat16)] * 3
+        + [pltpu.SemaphoreType.DMA((rows,))] * 4,
+        compiler_params=pltpu.CompilerParams(collective_id=2, has_side_effects=True),
+    )(pick, full_t, gate, up, down)
 
 
 def sum_kernel(
@@ -250,22 +349,15 @@
     slot = jnp.sum(onehot * jnp.cumsum(onehot, axis=0), axis=1) - 1
     place = jnp.where(flat_ids % 2 == which, (flat_ids // 2) * capacity + slot, slots)
     place = place.reshape(count_tok, topk).T
-    targets = jnp.arange(slots, dtype=jnp.int32)
+    turn = jnp.arange(slots, dtype=jnp.int32)
+    peer = (lax.axis_index("row") + mixed(turn // capacity, rows_count)) % rows_count
+    targets = peer * capacity + turn % capacity
     hit = targets[:, None, None] == place[None, :, :]
     dispatch = jnp.any(hit, axis=1).astype(jnp.bfloat16)
     combine = jnp.sum(jnp.where(hit, gate_vals.T[None, :, :], jnp.float32(0.0)), axis=1)
     combine = jnp.concatenate(split_pair(combine), axis=1)
 
-    outgoing = contract(dispatch, full_t, 1, 1).astype(jnp.bfloat16)
-    outgoing = outgoing.reshape(rows_count, capacity, features)
-    mine = lax.all_to_all(outgoing, "row", split_axis=0, concat_axis=0, tiled=True)
-    mine = mine.reshape(slots, features)
-    gate = contract(mine, w_gate[0], 1, 1)
-    upper = contract(mine, w_up[0], 1, 1)
-    hidden = (jax.nn.silu(gate) * upper).astype(jnp.bfloat16)
-    partial_out = contract(hidden, w_down[0], 1, 0).astype(jnp.bfloat16)
-    partial_out = partial_out.reshape(rows_count, capacity, features)
-    returned = lax.all_to_all(partial_out, "row", split_axis=0, concat_axis=0, tiled=True)
+    returned = run_experts(dispatch, full_t, w_gate[0], w_up[0], w_down[0])
     returned = returned.reshape(slots, features)
     routed_t = contract(returned, combine, 0, 0)
     routed_t = routed_t[:, :count_tok] + routed_t[:, count_tok:]

time: 173 us -> 163 us (0.942)
  the two profiles are of different devices: /device:TPU:8 before, /device:TPU:16 now
where the time goes in v3:
time: 163 us; the launch traced here: 162 us
  Pallas kernels  145 us (89%)
  other arithmetic  8.22 us (5%)
  matrix products  5.36 us (3%)
  local copies, waits for them, and re-layouts  3.54 us (2%)
    pallas_call x1, Pallas kernels, run_experts(): pl.pallas_call(functools.partial(expert_kernel, rows, groups), out_shape=...  70.6 us
    pallas_call x1, Pallas kernels, gather(): pl.pallas_call(functools.partial(gather_kernel, rows, cols), out_shape=(j...  42.6 us
    pallas_call x1, Pallas kernels, sum_shares(): pl.pallas_call(functools.partial(sum_kernel, cols), out_shape=(jax.ShapeD...  32 us
    dot_general x3, matrix products, contract(): lax.dot_general(left, right, (((left_dim,), (right_dim,)), ((), ())), pre...  5.36 us

profile of v3, /device:TPU:16, one launch (start us, length us, event | category | flops | bytes accessed | tf_op | source)
XLA Modules:
  0.0 162.4 jit_solution(14625335385308746401)
XLA Ops:
  0.0 0.0 copy-start.1
  0.0 0.7 copy.30
  0.8 0.1 reduce.1
  0.9 0.7 convert_reduce_fusion
  1.7 0.7 select_reduce_fusion
  2.4 1.4 pad_maximum_fusion.maps_ref
  3.8 0.8 copy.22
  4.6 0.1 eq.89
  4.7 0.1 eq.85
  4.9 1.8 %reduce-window.18 = s32[64,6,128]{2,0,1:T(8,128)S(1)} reduce-window(s32[64,6,128]{2,0,1:T(8,128)S(1)} %fusion.12, s32[]{:T(128)} %constant.100.clone.1), window={size=1x1x128 pad=0_0x0_0x127_0}, to_apply=%region_0.1 | reduce-window | flops 6242304 | bytes 393220 | tf_op jit(solution)/shard_map/reduce-window
  6.7 0.3 slice_reduce_fusion
  7.0 0.1 fusion.11
  7.1 0.1 sub.29
  7.3 0.1 fusion.17
  7.3 0.1 copy.29
  7.4 0.3 compare_reduce_fusion
  7.7 0.0 copy-start
  7.7 0.7 convert_element_type.27.pick_ref
  8.3 0.0 copy-done.1
  8.4 0.2 fusion
  8.6 42.6 %shard_map.109 = (bf16[16,160,128]{2,1,0:T(8,128)(2,1)}, bf16[32,64,160]{2,1,0:T(8,128)(2,1)}) custom-call(bf16[160,128]{1,0:T(8,128)(2,1)} %bitcast.52, bf16[64,160]{1,0:T(8,128)(2,1)} %pad_maximum_fusion.maps_ref), custom_call_target="tpu_custom_call" | custom-call | tf_op jit(solution)/shard_map/pallas_call | solution.py:113
  51.2 1.3 fusion.35
  52.5 0.0 copy-done
  52.5 0.9 fusion.1.low_ref
  53.4 70.6 %shard_map.110 = bf16[32,16,2560]{2,1,0:T(8,128)(2,1)} custom-call(bf16[512,128]{1,0:T(8,128)(2,1)} %convert_element_type.27.pick_ref, bf16[2560,128]{1,0:T(8,128)(2,1)} %bitcast.50, bf16[192,2560]{1,0:T(8,128)(2,1)} %bitcast.47, bf16[192,2560]{1,0:T(8,128)(2,1)} %bitcast.48, bf16[192,2560]{1,0:T(8,128)(2,1)} %bitcast.49), custom_call_target="tpu_custom_call" | custom-call | tf_op jit(solution)/shard_map/pallas_call | solution.py:218
  124.0 2.6 %fusion.6 = f32[2560,256]{1,0:T(8,128)S(1)} fusion(bf16[512,2560]{1,0:T(8,128)(2,1)} %bitcast.42, bf16[512,128]{1,0:T(8,128)(2,1)S(1)} %get-tuple-element.16, bf16[512,128]{1,0:T(8,128)(2,1)S(1)} %get-tuple-element.15), kind=kOutput, calls=%fused_computation.13 | convolution fusion | flops 671612928 | bytes 5505024 | tf_op jit(solution)/shard_map/dot_general | solution.py:18
  126.6 1.2 slice_add_fusion
  127.8 32.0 %shard_map.111 = (f32[160,128]{1,0:T(8,128)}, f32[16,128]{1,0:T(8,128)}) custom-call(f32[16,160,128]{2,1,0:T(8,128)} %bitcast.43, f32[16,128]{1,0:T(8,128)} %fusion.1.low_ref), custom_call_target="tpu_custom_call" | custom-call | tf_op jit(solution)/shard_map/pallas_call | solution.py:293
  159.8 0.7 convert_element_type.31
  160.5 0.1 broadcast_select_fusion
  160.5 1.8 %fusion.4 = bf16[128,160]{0,1:T(8,128)(2,1)} fusion(f32[160,128]{1,0:T(8,128)} %get-tuple-element.11, bf16[1024,160]{1,0:T(8,128)(2,1)S(1)} %bitcast.44, bf16[1024,128]{1,0:T(8,128)(2,1)S(1)} %bitcast.45), kind=kOutput, calls=%fused_computation.9 | convolution fusion | flops 42004480 | bytes 712704 | tf_op jit(solution)/shard_map/dot_general | solution.py:18
  (7 shorter events, 0.2 us)
Async XLA Ops:
  0.0 8.4 %copy-start.1 = (f32[128,6]{0,1:T(8,128)S(1)}, f32[128,6]{0,1:T(8,128)}, u32[]{:S(2)}) copy-start(f32[128,6]{0,1:T(8,128)} %param.18) | copy-start | bytes 9220
  7.7 44.8 %copy-start = (bf16[128,160]{0,1:T(8,128)(2,1)S(1)}, bf16[128,160]{0,1:T(8,128)(2,1)}, u32[]{:S(2)}) copy-start(bf16[128,160]{0,1:T(8,128)(2,1)} %param.11) | copy-start | bytes 122884

commit v4 on v2

--- a/solution.py
+++ b/solution.py
@@ -1,4 +1,5 @@
 import functools
+import math
 
 import jax
 import jax.numpy as jnp
@@ -17,11 +18,6 @@
     return lax.dot_general(
         left, right, (((left_dim,), (right_dim,)), ((), ())), preferred_element_type=jnp.float32
     )
-
-
-def split_pair(value):
-    high = lax.reduce_precision(value, 8, 7)
-    return high.astype(jnp.bfloat16), (value - high).astype(jnp.bfloat16)
 
 
 def remote(src, dst, send_sem, recv_sem, axis_name, peer):
@@ -35,12 +31,28 @@
     )
 
 
-def gather_kernel(
-    rows, cols, tok_ref, maps_ref, full_ref, all_ref, own_sem, ring_send, ring_recv, row_send, row_recv
+def mixed(turn, rows):
+    return turn * (13 if math.gcd(13, rows) == 1 else 1) % rows
+
+
+def expert_kernel(
+    rows, cols, groups,
+    tok_ref, adp_down_ref, adp_up_ref, ids_ref, vals_ref, perm_ref, lengths_ref, req_ref,
+    gate_hbm, up_hbm, down_hbm,
+    back_ref, comb_ref, all_ref, low_ref, adapter_ref,
+    full_ref, maps_ref, pick_ref, out_buf, in_buf, part_buf, gate_ref, up_ref, down_ref,
+    own_sem, ring_send, ring_recv, row_send, row_recv, out_send, out_recv, back_send, back_recv,
 ):
     me_r, me_c = lax.axis_index("row"), lax.axis_index("col")
     sides = (lax.rem(me_c + 1, cols), lax.rem(me_c + cols - 1, cols))
     hops = (cols // 2, cols - 1 - cols // 2)
+    members = rows // groups
+    capacity, features = back_ref.shape[1:]
+    share, count_tok = tok_ref.shape
+    topk = ids_ref.shape[0]
+    height = members * capacity
+    joined = math.gcd(cols, 4)
+    width = joined * share
 
     barrier = pltpu.get_barrier_semaphore()
     for side in sides:
@@ -52,7 +64,17 @@
         return carry
 
     lax.fori_loop(1, rows, greet, 0)
-    pl.semaphore_wait(barrier, rows + 1)
+
+    weights = (
+        pltpu.make_async_copy(gate_hbm, gate_ref, own_sem.at[2]),
+        pltpu.make_async_copy(up_hbm, up_ref, own_sem.at[3]),
+        pltpu.make_async_copy(down_hbm, down_ref, own_sem.at[4]),
+    )
+    for copy in weights:
+        copy.start()
+    kept = adp_down_ref.shape[0]
+    maps_ref[:kept] = adp_down_ref[...]
+    maps_ref[kept:] = adp_up_ref[...]
 
     def shard(way, step):
         return lax.rem(me_c + cols - step, cols) if way == 0 else lax.rem(me_c + step, cols)
@@ -71,60 +93,195 @@
         peer = lax.rem(me_r + away, rows)
         return remote(maps_ref, at, row_send.at[away], row_recv.at[away], "row", peer)
 
+    def outward(turn):
+        peer = lax.rem(me_r + mixed(turn, rows), rows)
+        return remote(
+            out_buf.at[turn], in_buf.at[turn], out_send.at[turn], out_recv.at[turn], "row", peer
+        )
+
+    def homeward(turn):
+        peer = lax.rem(me_r + rows - mixed(turn, rows), rows)
+        return remote(
+            part_buf.at[turn], back_ref.at[turn], back_send.at[turn], back_recv.at[turn], "row", peer
+        )
+
+    def turns(group):
+        return [turn for turn in range(group * members, (group + 1) * members) if turn > 0]
+
+    pl.semaphore_wait(barrier, rows + 1)
     for way in range(2):
         sending(way, 0).start()
-
-    def row_start(away, carry):
-        row_copy(away, me_r).start()
-        return carry
-
-    lax.fori_loop(1, rows, row_start, 0)
     own = (
         pltpu.make_async_copy(tok_ref, full_ref.at[me_c], own_sem.at[0]),
         pltpu.make_async_copy(maps_ref, all_ref.at[me_r], own_sem.at[1]),
     )
     for copy in own:
         copy.start()
+
+    turn_at = lax.broadcasted_iota(jnp.int32, (rows, count_tok), 0)
+    peer_at = lax.rem(me_r + mixed(turn_at, rows), rows)
+    expert_at = 2 * peer_at + me_c // (cols // 2)
+    named = jnp.zeros((rows, count_tok), jnp.float32)
+    value = jnp.zeros((rows, count_tok), jnp.float32)
+    for k in range(topk):
+        same = ids_ref[k : k + 1, :] == expert_at
+        named = named + jnp.where(same, 1.0, 0.0)
+        value = value + jnp.where(same, vals_ref[k : k + 1, :], 0.0)
+    earlier = lax.broadcasted_iota(jnp.int32, (count_tok, count_tok), 0)
+    later = lax.broadcasted_iota(jnp.int32, (count_tok, count_tok), 1)
+    before = jnp.where(earlier < later, 1.0, 0.0).astype(jnp.bfloat16)
+    slot = contract(named.astype(jnp.bfloat16), before, 1, 0).astype(jnp.int32)
+    slot = jnp.where(named > 0.0, slot, capacity)
+    place = lax.broadcasted_iota(jnp.int32, (rows, capacity, count_tok), 1)
+    hit = place == slot[:, None, :]
+    pick_ref[...] = (
+        jnp.where(hit, 1.0, 0.0).reshape(rows * capacity, count_tok).astype(jnp.bfloat16)
+    )
+    comb = jnp.where(hit, value[:, None, :], 0.0).reshape(rows * capacity, count_tok)
+    high = comb.astype(jnp.bfloat16)
+    comb_ref[:, :count_tok] = high
+    comb_ref[:, count_tok:] = (comb - high.astype(jnp.float32)).astype(jnp.bfloat16)
+
+    end = jnp.int32(0)
+    request = jnp.zeros((1, count_tok), jnp.int32)
+    for i in range(lengths_ref.shape[0]):
+        end = end + lengths_ref[i]
+        request = request + jnp.where(perm_ref[...] >= end, 1, 0)
+    adapter = jnp.zeros((1, count_tok), jnp.int32)
+    for i in range(lengths_ref.shape[0]):
+        adapter = adapter + jnp.where(request == i, req_ref[i], 0)
+    adapter_ref[...] = adapter
+
+    batch = -(-(rows - 1) // max(hops))
     for step in range(max(hops)):
         for way in range(2):
             if step < hops[way]:
                 arriving(way, step).wait_recv()
                 if step + 1 < hops[way]:
                     sending(way, step + 1).start()
+        for turn in range(1 + step * batch, min(rows, 1 + (step + 1) * batch)):
+            row_copy(mixed(turn, rows), me_r).start()
     for copy in own:
         copy.wait()
+
+    for group in range(groups):
+        first = group * members
+        picks = pick_ref[group * height : (group + 1) * height, :]
+
+        def fill(tile, carry):
+            at = pl.multiple_of(tile * width, width)
+            piece = full_ref[pl.ds(tile * joined, joined)].reshape(width, count_tok)
+            block = contract(picks, piece, 1, 1).astype(jnp.bfloat16)
+            out_buf[first : first + members, :, pl.ds(at, width)] = block.reshape(
+                members, capacity, width
+            )
+            return carry
+
+        lax.fori_loop(0, features // width, fill, 0)
+        for turn in turns(group):
+            outward(turn).start()
+    in_buf[0] = out_buf[0]
+
+    def row_end(away, carry):
+        row_copy(away, lax.rem(me_r + rows - away, rows)).wait_recv()
+        return carry
+
+    lax.fori_loop(1, rows, row_end, 0)
+    rank = low_ref.shape[0]
+    own_adapters = kept // rank
+    low_ref[...] = jnp.zeros_like(low_ref)
+
+    def project(owner, carry):
+        piece = all_ref[owner][:kept]
+        projected = contract(piece, tok_ref[...], 1, 0)
+        for i in range(own_adapters):
+            chosen = adapter == owner * own_adapters + i
+            low_ref[...] += jnp.where(chosen, projected[i * rank : (i + 1) * rank], 0.0)
+        return carry
+
+    lax.fori_loop(0, rows, project, 0)
+
+    for copy in weights:
+        copy.wait()
+    for group in range(groups):
+        first = group * members
+        for turn in turns(group):
+            outward(turn).wait_recv()
+        mine = in_buf[first : first + members].reshape(height, features)
+        gate = contract(mine, gate_ref[...], 1, 1)
+        upper = contract(mine, up_ref[...], 1, 1)
+        hidden = (jax.nn.silu(gate) * upper).astype(jnp.bfloat16)
+
+        def fill_part(tile, carry):
+            at = pl.multiple_of(tile * width, width)
+            block = contract(hidden, down_ref[:, pl.ds(at, width)], 1, 0).astype(jnp.bfloat16)
+            part_buf[first : first + members, :, pl.ds(at, width)] = block.reshape(
+                members, capacity, width
+            )
+            return carry
+
+        lax.fori_loop(0, features // width, fill_part, 0)
+        for turn in turns(group):
+            homeward(turn).start()
+    back_ref[0] = part_buf[0]
+    for turn in range(1, rows):
+        homeward(turn).wait_recv()
     for way in range(2):
         for step in range(hops[way]):
             sending(way, step).wait_send()
 
-    def row_end(away, carry):
-        copy = row_copy(away, lax.rem(me_r + rows - away, rows))
-        copy.wait_recv()
-        copy.wait_send()
+    def row_sent(away, carry):
+        row_copy(away, me_r).wait_send()
         return carry
 
-    lax.fori_loop(1, rows, row_end, 0)
-
-
-def gather(tokens_t, maps):
+    lax.fori_loop(1, rows, row_sent, 0)
+    for turn in range(1, rows):
+        outward(turn).wait_send()
+        homeward(turn).wait_send()
+
+
+def run_experts(
+    capacity, tokens_t, adp_down, adp_up, ids, vals, perm, lengths, req_adapter, gate, up, down
+):
     rows, cols = lax.axis_size("row"), lax.axis_size("col")
+    share, count_tok = tokens_t.shape
+    features = gate.shape[1]
+    blocks = (rows, capacity, features)
+    slots = rows * capacity
+    rank = adp_down.shape[1]
+    adp_down, adp_up = adp_down.reshape(-1, share), adp_up.reshape(-1, share)
+    maps = (2 * adp_down.shape[0], share)
+    groups = math.gcd(rows, 4)
+    smem = pl.BlockSpec(memory_space=pltpu.SMEM)
+    hbm = pl.BlockSpec(memory_space=pl.ANY)
     return pl.pallas_call(
-        functools.partial(gather_kernel, rows, cols),
+        functools.partial(expert_kernel, rows, cols, groups),
         out_shape=(
-            jax.ShapeDtypeStruct((cols,) + tokens_t.shape, tokens_t.dtype),
-            jax.ShapeDtypeStruct((rows,) + maps.shape, maps.dtype),
+            jax.ShapeDtypeStruct(blocks, jnp.bfloat16),
+            jax.ShapeDtypeStruct((slots, 2 * count_tok), jnp.bfloat16),
+            jax.ShapeDtypeStruct((rows,) + maps, jnp.bfloat16),
+            jax.ShapeDtypeStruct((rank, count_tok), jnp.float32),
+            jax.ShapeDtypeStruct((1, count_tok), jnp.int32),
         ),
-        in_specs=[VMEM] * 2,
-        out_specs=(VMEM, VMEM),
+        in_specs=[VMEM] * 6 + [smem] * 2 + [hbm] * 3,
+        out_specs=(VMEM,) * 5,
         scratch_shapes=[
-            pltpu.SemaphoreType.DMA((2,)),
+            pltpu.VMEM((cols, share, count_tok), jnp.bfloat16),
+            pltpu.VMEM(maps, jnp.bfloat16),
+            pltpu.VMEM((slots, count_tok), jnp.bfloat16),
+            pltpu.VMEM(blocks, jnp.bfloat16),
+            pltpu.VMEM(blocks, jnp.bfloat16),
+            pltpu.VMEM(blocks, jnp.bfloat16),
+            pltpu.VMEM(gate.shape, jnp.bfloat16),
+            pltpu.VMEM(up.shape, jnp.bfloat16),
+            pltpu.VMEM(down.shape, jnp.bfloat16),
+            pltpu.SemaphoreType.DMA((5,)),
             pltpu.SemaphoreType.DMA((2, cols)),
             pltpu.SemaphoreType.DMA((2, cols)),
-            pltpu.SemaphoreType.DMA((rows,)),
-            pltpu.SemaphoreType.DMA((rows,)),
-        ],
+        ]
+        + [pltpu.SemaphoreType.DMA((rows,))] * 6,
         compiler_params=pltpu.CompilerParams(collective_id=0, has_side_effects=True),
-    )(tokens_t, maps)
+    )(tokens_t, adp_down, adp_up, ids, vals, perm, lengths, req_adapter, gate, up, down)
 
 
 def sum_kernel(
@@ -228,63 +385,21 @@
     rows_count = lax.axis_size("row")
     cols_count = lax.axis_size("col")
     experts = 2 * rows_count
-    parts = cols_count // 2
-    which = lax.axis_index("col") // parts
     topk = expert_ids.shape[1]
     capacity = max(2, (4 * count_tok * topk + 3 * experts - 1) // (3 * experts))
     slots = rows_count * capacity
-    features = cols_count * share
     rank = adp_down.shape[1]
     own_adapters = adp_down.shape[0]
     adapters = own_adapters * rows_count
 
-    tokens_t = tokens.T
-    maps = jnp.concatenate(
-        [adp_down.reshape(own_adapters * rank, share), adp_up.reshape(own_adapters * rank, share)]
-    )
-    full_t, maps = gather(tokens_t, maps)
-    full_t = full_t.reshape(features, count_tok)
-
-    flat_ids = expert_ids.reshape(-1)
-    onehot = (flat_ids[:, None] == jnp.arange(experts, dtype=jnp.int32)[None, :]).astype(jnp.int32)
-    slot = jnp.sum(onehot * jnp.cumsum(onehot, axis=0), axis=1) - 1
-    place = jnp.where(flat_ids % 2 == which, (flat_ids // 2) * capacity + slot, slots)
-    place = place.reshape(count_tok, topk).T
-    targets = jnp.arange(slots, dtype=jnp.int32)
-    hit = targets[:, None, None] == place[None, :, :]
-    dispatch = jnp.any(hit, axis=1).astype(jnp.bfloat16)
-    combine = jnp.sum(jnp.where(hit, gate_vals.T[None, :, :], jnp.float32(0.0)), axis=1)
-    combine = jnp.concatenate(split_pair(combine), axis=1)
-
-    outgoing = contract(dispatch, full_t, 1, 1).astype(jnp.bfloat16)
-    outgoing = outgoing.reshape(rows_count, capacity, features)
-    mine = lax.all_to_all(outgoing, "row", split_axis=0, concat_axis=0, tiled=True)
-    mine = mine.reshape(slots, features)
-    gate = contract(mine, w_gate[0], 1, 1)
-    upper = contract(mine, w_up[0], 1, 1)
-    hidden = (jax.nn.silu(gate) * upper).astype(jnp.bfloat16)
-    partial_out = contract(hidden, w_down[0], 1, 0).astype(jnp.bfloat16)
-    partial_out = partial_out.reshape(rows_count, capacity, features)
-    returned = lax.all_to_all(partial_out, "row", split_axis=0, concat_axis=0, tiled=True)
-    returned = returned.reshape(slots, features)
-    routed_t = contract(returned, combine, 0, 0)
+    returned, combine, maps, partial_low, adapter = run_experts(
+        capacity, tokens.T, adp_down, adp_up, expert_ids.T, gate_vals.T, perm[None],
+        lengths, req_adapter, w_gate[0], w_up[0], w_down[0],
+    )
+    routed_t = contract(returned.reshape(slots, -1), combine, 0, 0)
     routed_t = routed_t[:, :count_tok] + routed_t[:, count_tok:]
-
-    maps = maps.reshape(rows_count, 2, own_adapters * rank, share)
-    down_all = maps[:, 0].reshape(adapters * rank, share)
-    up_all = maps[:, 1].reshape(adapters * rank, share)
-    nreq = lengths.shape[0]
-    ends = jnp.cumsum(lengths)
-    request = jnp.sum((perm[:, None] >= ends[None, :]).astype(jnp.int32), axis=1)
-    adapter = jnp.sum(
-        jnp.where(
-            request[:, None] == jnp.arange(nreq, dtype=jnp.int32)[None, :], req_adapter[None, :], 0
-        ),
-        axis=1,
-    )
-    chosen = jnp.arange(adapters, dtype=jnp.int32)[:, None, None] == adapter[None, None, :]
-    projected = contract(down_all, tokens_t, 1, 0).reshape(adapters, rank, count_tok)
-    partial_low = jnp.sum(jnp.where(chosen, projected, jnp.float32(0.0)), axis=0)
+    up_all = maps[:, own_adapters * rank :].reshape(adapters * rank, share)
+    chosen = jnp.arange(adapters, dtype=jnp.int32)[:, None, None] == adapter[None]
 
     total, low = sum_shares(routed_t.reshape(cols_count, share, count_tok), partial_low)
     low = low.astype(jnp.bfloat16)

time: 173 us -> 143 us (0.83)
  the two profiles are of different devices: /device:TPU:8 before, /device:TPU:26 now
where the time goes in v4:
time: 143 us; the launch traced here: 142 us
  Pallas kernels  136 us (95%)
  matrix products  4.45 us (3%)
  other arithmetic  1.95 us (1%)
    pallas_call x1, Pallas kernels, run_experts(): pl.pallas_call(functools.partial(expert_kernel, rows, cols, groups), out_...  102 us
    pallas_call x1, Pallas kernels, sum_shares(): pl.pallas_call(functools.partial(sum_kernel, cols), out_shape=(jax.ShapeD...  34.2 us
    dot_general x2, matrix products, contract(): lax.dot_general(left, right, (((left_dim,), (right_dim,)), ((), ())), pre...  4.45 us

profile of v4, /device:TPU:26, one launch (start us, length us, event | category | flops | bytes accessed | tf_op | source)
XLA Modules:
  0.0 142.3 jit_solution(9142127101869256133)
XLA Ops:
  0.0 101.6 %shard_map.109 = (bf16[32,16,2560]{2,1,0:T(8,128)(2,1)}, bf16[512,256]{1,0:T(8,128)(2,1)}, bf16[32,64,160]{2,1,0:T(8,128)(2,1)}, f32[16,128]{1,0:T(8,128)}, s32[1,128]{1,0:T(1,128)}) custom-call(bf16[160,128]{1,0:T(8,128)(2,1)} %bitcast.27, bf16[32,160]{1,0:T(8,128)(2,1)} %bitcast.28, bf16[32,160]{1,0:T(8,128)(2,1)} %bitcast.29, s32[6,128]{1,0:T(8,128)} %bitcast.30, ...), custom_call_target="tpu_custom_call" | custom-call | tf_op jit(solution)/shard_map/pallas_call | solution.py:257
  101.6 2.6 %fusion.3 = f32[2560,256]{1,0:T(8,128)S(1)} fusion(bf16[512,2560]{1,0:T(8,128)(2,1)} %bitcast.21, bf16[512,256]{1,0:T(8,128)(2,1)} %get-tuple-element.13), kind=kOutput, calls=%fused_computation.7 | convolution fusion | flops 671088640 | bytes 5505024 | tf_op jit(solution)/shard_map/dot_general | solution.py:18
  104.2 0.0 copy-start.1
  104.2 0.0 copy-start
  104.2 1.2 slice_add_fusion
  105.4 34.2 %shard_map.110 = (f32[160,128]{1,0:T(8,128)}, f32[16,128]{1,0:T(8,128)}) custom-call(f32[16,160,128]{2,1,0:T(8,128)} %bitcast.20, f32[16,128]{1,0:T(8,128)} %get-tuple-element.14.low_ref), custom_call_target="tpu_custom_call" | custom-call | tf_op jit(solution)/shard_map/pallas_call | solution.py:351
  139.6 0.7 convert_element_type.9
  140.3 0.0 copy-done.1
  140.3 0.1 broadcast_select_fusion
  140.4 0.0 copy-done
  140.4 1.8 %fusion.2 = bf16[128,160]{0,1:T(8,128)(2,1)} fusion(f32[160,128]{1,0:T(8,128)} %get-tuple-element.15, bf16[1024,160]{1,0:T(8,128)(2,1)S(1)} %bitcast.22, bf16[1024,128]{1,0:T(8,128)(2,1)S(1)} %bitcast.23), kind=kOutput, calls=%fused_computation.4 | convolution fusion | flops 42004480 | bytes 712704 | tf_op jit(solution)/shard_map/dot_general | solution.py:18
  (2 shorter events, 0.0 us)
Async XLA Ops:
  104.2 36.1 %copy-start.1 = (s32[1,128]{1,0:T(1,128)S(1)}, s32[1,128]{1,0:T(1,128)}, u32[]{:S(2)}) copy-start(s32[1,128]{1,0:T(1,128)} %get-tuple-element.17) | copy-start | bytes 1540
  104.2 36.2 %copy-start = (bf16[32,64,160]{2,1,0:T(8,128)(2,1)S(1)}, bf16[32,64,160]{2,1,0:T(8,128)(2,1)}, u32[]{:S(2)}) copy-start(bf16[32,64,160]{2,1,0:T(8,128)(2,1)} %get-tuple-element.16) | copy-start | bytes 1966084

commit v5 on v4

v5 whole, which is shorter than its diff:
```python
import functools
import math

import jax
import jax.numpy as jnp
from jax import lax
from jax.experimental import pallas as pl
from jax.experimental.pallas import tpu as pltpu
from jax.sharding import PartitionSpec as P

MESH = pl.DeviceIdType.MESH
VMEM = pl.BlockSpec(memory_space=pltpu.VMEM)

adapter_scale_factor = 2.0


def contract(left, right, left_dim, right_dim):
    return lax.dot_general(
        left, right, (((left_dim,), (right_dim,)), ((), ())), preferred_element_type=jnp.float32
    )


def remote(src, dst, send_sem, recv_sem, axis_name, peer):
    return pltpu.make_async_remote_copy(
        src_ref=src,
        dst_ref=dst,
        send_sem=send_sem,
        recv_sem=recv_sem,
        device_id={axis_name: peer},
        device_id_type=MESH,
    )


def mixed(turn, rows):
    return lax.rem(turn * (13 if math.gcd(13, rows) == 1 else 1), rows)


def expert_kernel(
    rows, cols, groups,
    tok_ref, adp_down_ref, adp_up_ref, ids_ref, vals_ref, perm_ref, lengths_ref, req_ref,
    gate_hbm, up_hbm, down_hbm,
    total_ref, low_total_ref, all_ref, adapter_ref,
    full_ref, maps_ref, pick_ref, comb_ref, out_buf, in_buf, part_buf, back_buf,
    gate_ref, up_ref, down_ref, gate_t, up_t, down_t, gate_acc, up_acc, low_ref, share_part,
    sum_out, sum_in, low_out, low_in,
    own_sem, ring_send, ring_recv, row_send, row_recv, out_send, out_recv, back_send, back_recv,
    sum_send, sum_recv, low_send, low_recv,
):
    me_r, me_c = lax.axis_index("row"), lax.axis_index("col")
    sides = (lax.rem(me_c + 1, cols), lax.rem(me_c + cols - 1, cols))
    hops = (cols // 2, cols - 1 - cols // 2)
    capacity, features = back_buf.shape[1:]
    slots = rows * capacity
    hidden_units = gate_ref.shape[0]
    share, count_tok = tok_ref.shape
    topk = ids_ref.shape[0]
    width = features // groups
    offsets = [(-2 * g - 1, -2 * g - 2, 2 * g, 2 * g + 1) for g in range(groups)]
    where = {off % cols: 4 * g + i for g in range(groups) for i, off in enumerate(offsets[g])}

    barrier = pltpu.get_barrier_semaphore()
    for side in sides:
        pl.semaphore_signal(barrier, inc=1, device_id={"col": side}, device_id_type=MESH)

    def greet(away, carry):
        peer = lax.rem(me_r + away, rows)
        pl.semaphore_signal(barrier, inc=1, device_id={"row": peer}, device_id_type=MESH)
        return carry

    lax.fori_loop(1, rows, greet, 0)

    weights = (
        pltpu.make_async_copy(gate_hbm, gate_ref, own_sem.at[2]),
        pltpu.make_async_copy(up_hbm, up_ref, own_sem.at[3]),
        pltpu.make_async_copy(down_hbm, down_ref, own_sem.at[4]),
    )
    for copy in weights:
        copy.start()
    kept = adp_down_ref.shape[0]
    maps_ref[:kept] = adp_down_ref[...]
    maps_ref[kept:] = adp_up_ref[...]

    def share_at(off):
        return lax.rem(me_c + cols + off, cols)

    def shard(way, step):
        return share_at(-step) if way == 0 else share_at(step)

    def sending(way, step):
        at = full_ref.at[shard(way, step)]
        src = tok_ref if step == 0 else at
        return remote(src, at, ring_send.at[way, step], ring_recv.at[way, step], "col", sides[way])

    def arriving(way, step):
        at = full_ref.at[shard(way, step + 1)]
        return remote(at, at, ring_send.at[way, step], ring_recv.at[way, step], "col", sides[way])

    def row_copy(away, owner):
        at = all_ref.at[owner]
        peer = lax.rem(me_r + away, rows)
        return remote(maps_ref, at, row_send.at[away], row_recv.at[away], "row", peer)

    def lanes(group):
        return pl.ds(group * width, width)

    def outward(group, turn):
        peer = lax.rem(me_r + mixed(turn, rows), rows)
        return remote(
            out_buf.at[turn, :, lanes(group)], in_buf.at[turn, :, lanes(group)],
            out_send.at[group, turn], out_recv.at[group, turn], "row", peer,
        )

    def homeward(group, turn):
        peer = lax.rem(me_r + rows - mixed(turn, rows), rows)
        return remote(
            part_buf.at[turn, :, lanes(group)], back_buf.at[turn, :, lanes(group)],
            back_send.at[group, turn], back_recv.at[group, turn], "row", peer,
        )

    def each_turn(do):
        def step(turn, carry):
            do(turn)
            return carry

        lax.fori_loop(1, rows, step, 0)

    def joined(ref, group):
        return jnp.concatenate([ref[share_at(off)] for off in offsets[group]], axis=0)

    pl.semaphore_wait(barrier, rows + 1)
    for way in range(2):
        sending(way, 0).start()
    own = (
        pltpu.make_async_copy(tok_ref, full_ref.at[me_c], own_sem.at[0]),
        pltpu.make_async_copy(maps_ref, all_ref.at[me_r], own_sem.at[1]),
    )
    for copy in own:
        copy.start()

    turn_at = lax.broadcasted_iota(jnp.int32, (rows, count_tok), 0)
    peer_at = lax.rem(me_r + mixed(turn_at, rows), rows)
    expert_at = 2 * peer_at + me_c // (cols // 2)
    named = jnp.zeros((rows, count_tok), jnp.float32)
    value = jnp.zeros((rows, count_tok), jnp.float32)
    for k in range(topk):
        same = ids_ref[k : k + 1, :] == expert_at
        named = named + jnp.where(same, 1.0, 0.0)
        value = value + jnp.where(same, vals_ref[k : k + 1, :], 0.0)
    earlier = lax.broadcasted_iota(jnp.int32, (count_tok, count_tok), 0)
    later = lax.broadcasted_iota(jnp.int32, (count_tok, count_tok), 1)
    before = jnp.where(earlier < later, 1.0, 0.0).astype(jnp.bfloat16)
    slot = contract(named.astype(jnp.bfloat16), before, 1, 0).astype(jnp.int32)
    slot = jnp.where(named > 0.0, slot, capacity)
    place = lax.broadcasted_iota(jnp.int32, (rows, capacity, count_tok), 1)
    hit = place == slot[:, None, :]
    pick_ref[...] = (
        jnp.where(hit, 1.0, 0.0).reshape(rows * capacity, count_tok).astype(jnp.bfloat16)
    )
    comb = jnp.where(hit, value[:, None, :], 0.0).reshape(rows * capacity, count_tok)
    high = comb.astype(jnp.bfloat16)
    comb_ref[:, :count_tok] = high
    comb_ref[:, count_tok:] = (comb - high.astype(jnp.float32)).astype(jnp.bfloat16)

    end = jnp.int32(0)
    request = jnp.zeros((1, count_tok), jnp.int32)
    for i in range(lengths_ref.shape[0]):
        end = end + lengths_ref[i]
        request = request + jnp.where(perm_ref[...] >= end, 1, 0)
    adapter = jnp.zeros((1, count_tok), jnp.int32)
    for i in range(lengths_ref.shape[0]):
        adapter = adapter + jnp.where(request == i, req_ref[i], 0)
    adapter_ref[...] = adapter

    for copy in own:
        copy.wait()

    def ring_step(way, step):
        if step < hops[way]:
            arriving(way, step).wait_recv()
            if step + 1 < hops[way]:
                sending(way, step + 1).start()

    def accumulate(group):
        each_turn(lambda turn: outward(group, turn).wait_recv())
        mine = in_buf[:, :, group * width : (group + 1) * width].reshape(slots, width)
        for acc, weight in ((gate_acc, gate_t), (up_acc, up_t)):
            product = contract(mine, joined(weight, group), 1, 0)
            if group == 0:
                acc[...] = product
            else:
                acc[...] += product

    for group in range(groups):
        ring_step(0, 2 * group)
        if group > 0:
            ring_step(1, 2 * group - 1)
        ring_step(1, 2 * group)
        ring_step(0, 2 * group + 1)
        block = contract(pick_ref[...], joined(full_ref, group), 1, 1).astype(jnp.bfloat16)
        block = block.reshape(rows, capacity, width)
        out_buf[:, :, group * width : (group + 1) * width] = block
        in_buf[0, :, group * width : (group + 1) * width] = block[0]
        each_turn(lambda turn: outward(group, turn).start())
        if group == 0:
            for copy in weights:
                copy.wait()
            for plain, turned in ((gate_ref, gate_t), (up_ref, up_t), (down_ref, down_t)):
                for part in range(groups):
                    tile = plain[:, part * width : (part + 1) * width]
                    turned[4 * part : 4 * part + 4] = tile.T.reshape(4, share, hidden_units)
            each_turn(lambda turn: row_copy(mixed(turn, rows), me_r).start())
    for group in range(groups - 1):
        accumulate(group)

    def row_end(away, carry):
        row_copy(away, lax.rem(me_r + rows - away, rows)).wait_recv()
        return carry

    lax.fori_loop(1, rows, row_end, 0)
    rank = low_ref.shape[0]
    own_adapters = kept // rank
    low_ref[...] = jnp.zeros_like(low_ref)

    def project(owner, carry):
        piece = all_ref[owner][:kept]
        projected = contract(piece, tok_ref[...], 1, 0)
        for i in range(own_adapters):
            chosen = adapter == owner * own_adapters + i
            low_ref[...] += jnp.where(chosen, projected[i * rank : (i + 1) * rank], 0.0)
        return carry

    lax.fori_loop(0, rows, project, 0)

    accumulate(groups - 1)
    hidden = (jax.nn.silu(gate_acc[...]) * up_acc[...]).astype(jnp.bfloat16)
    for group in reversed(range(groups)):
        block = contract(hidden, joined(down_t, group), 1, 1).astype(jnp.bfloat16)
        block = block.reshape(rows, capacity, width)
        part_buf[:, :, group * width : (group + 1) * width] = block
        back_buf[0, :, group * width : (group + 1) * width] = block[0]
        each_turn(lambda turn: homeward(group, turn).start())

    sum_hops = (hops[1], hops[0])

    def sums(way, step):
        return (
            remote(
                sum_out.at[way, step], sum_in.at[way, step],
                sum_send.at[way, step], sum_recv.at[way, step], "col", sides[way],
            ),
            remote(
                low_out.at[way, step], low_in.at[way, step],
                low_send.at[way, step], low_recv.at[way, step], "col", sides[way],
            ),
        )

    def sum_step(way, step):
        off = sum_hops[0] - step if way == 0 else step - sum_hops[1]
        value, low = share_part[where[off % cols]], low_ref[...]
        if step > 0:
            for copy in sums(way, step - 1):
                copy.wait_recv()
            value = value + sum_in[way, step - 1].astype(jnp.float32)
            low = low + low_in[way, step - 1]
        sum_out[way, step] = value.astype(jnp.bfloat16)
        low_out[way, step] = low
        for copy in sums(way, step):
            copy.start()

    for step in range(sum_hops[1]):
        if step % 2 == 0:
            group = groups - 1 - step // 2
            each_turn(lambda turn: homeward(group, turn).wait_recv())
            back = back_buf[:, :, group * width : (group + 1) * width].reshape(slots, width)
            both = contract(back, comb_ref[...], 0, 0)
            both = both[:, :count_tok] + both[:, count_tok:]
            share_part[4 * group : 4 * group + 4] = both.reshape(4, share, count_tok)
        sum_step(1, step)
        if step > 0:
            sum_step(0, step - 1)
    total, low = share_part[where[0]], low_ref[...]
    for way in range(2):
        last = sum_hops[way] - 1
        for copy in sums(way, last):
            copy.wait_recv()
        total = total + sum_in[way, last].astype(jnp.float32)
        low = low + low_in[way, last]
    total_ref[...] = total
    low_total_ref[...] = low

    for way in range(2):
        for step in range(hops[way]):
            sending(way, step).wait_send()
        for step in range(sum_hops[way]):
            for copy in sums(way, step):
                copy.wait_send()
    each_turn(lambda turn: row_copy(turn, me_r).wait_send())
    for group in range(groups):
        each_turn(lambda turn: outward(group, turn).wait_send())
        each_turn(lambda turn: homeward(group, turn).wait_send())


def run_experts(
    capacity, tokens_t, adp_down, adp_up, ids, vals, perm, lengths, req_adapter, gate, up, down
):
    rows, cols = lax.axis_size("row"), lax.axis_size("col")
    share, count_tok = tokens_t.shape
    hidden_units, features = gate.shape
    blocks = (rows, capacity, features)
    slots = rows * capacity
    rank = adp_down.shape[1]
    adp_down, adp_up = adp_down.reshape(-1, share), adp_up.reshape(-1, share)
    maps = (2 * adp_down.shape[0], share)
    groups = cols // 4
    hops = cols // 2
    smem = pl.BlockSpec(memory_space=pltpu.SMEM)
    hbm = pl.BlockSpec(memory_space=pl.ANY)
    turned = pltpu.VMEM((cols, share, hidden_units), jnp.bfloat16)
    partial_low = pltpu.VMEM((2, hops, rank, count_tok), jnp.float32)
    return pl.pallas_call(
        functools.partial(expert_kernel, rows, cols, groups),
        out_shape=(
            jax.ShapeDtypeStruct((share, count_tok), jnp.float32),
            jax.ShapeDtypeStruct((rank, count_tok), jnp.float32),
            jax.ShapeDtypeStruct((rows,) + maps, jnp.bfloat16),
            jax.ShapeDtypeStruct((1, count_tok), jnp.int32),
        ),
        in_specs=[VMEM] * 6 + [smem] * 2 + [hbm] * 3,
        out_specs=(VMEM,) * 4,
        scratch_shapes=[
            pltpu.VMEM((cols, share, count_tok), jnp.bfloat16),
            pltpu.VMEM(maps, jnp.bfloat16),
            pltpu.VMEM((slots, count_tok), jnp.bfloat16),
            pltpu.VMEM((slots, 2 * count_tok), jnp.bfloat16),
        ]
        + [pltpu.VMEM(blocks, jnp.bfloat16)] * 4
        + [pltpu.VMEM(gate.shape, jnp.bfloat16)] * 3
        + [turned] * 3
        + [pltpu.VMEM((slots, hidden_units), jnp.float32)] * 2
        + [
            pltpu.VMEM((rank, count_tok), jnp.float32),
            pltpu.VMEM((cols, share, count_tok), jnp.float32),
            pltpu.VMEM((2, hops, share, count_tok), jnp.bfloat16),
            pltpu.VMEM((2, hops, share, count_tok), jnp.bfloat16),
            partial_low,
            partial_low,
            pltpu.SemaphoreType.DMA((5,)),
            pltpu.SemaphoreType.DMA((2, cols)),
            pltpu.SemaphoreType.DMA((2, cols)),
            pltpu.SemaphoreType.DMA((rows,)),
            pltpu.SemaphoreType.DMA((rows,)),
        ]
        + [pltpu.SemaphoreType.DMA((groups, rows))] * 4
        + [pltpu.SemaphoreType.DMA((2, hops))] * 4,
        compiler_params=pltpu.CompilerParams(collective_id=0, has_side_effects=True),
    )(tokens_t, adp_down, adp_up, ids, vals, perm, lengths, req_adapter, gate, up, down)


def body(
    tokens,
    w_gate,
    w_up,
    w_down,
    adp_down,
    adp_up,
    expert_ids,
    gate_vals,
    lengths,
    perm,
    req_adapter,
):
    count_tok = tokens.shape[0]
    share = tokens.shape[1]
    rows_count = lax.axis_size("row")
    experts = 2 * rows_count
    topk = expert_ids.shape[1]
    capacity = max(2, (4 * count_tok * topk + 3 * experts - 1) // (3 * experts))
    rank = adp_down.shape[1]
    own_adapters = adp_down.shape[0]
    adapters = own_adapters * rows_count

    total, low, maps, adapter = run_experts(
        capacity, tokens.T, adp_down, adp_up, expert_ids.T, gate_vals.T, perm[None],
        lengths, req_adapter, w_gate[0], w_up[0], w_down[0],
    )
    up_all = maps[:, own_adapters * rank :].reshape(adapters * rank, share)
    chosen = jnp.arange(adapters, dtype=jnp.int32)[:, None, None] == adapter[None]

    low = low.astype(jnp.bfloat16)
    expanded = jnp.where(chosen, low[None], jnp.bfloat16(0.0)).reshape(adapters * rank, count_tok)
    delta_t = contract(up_all, expanded, 0, 0)
    return (total + adapter_scale_factor * delta_t).T.astype(jnp.bfloat16)


def solution(mesh):
    in_specs = (
        P("row", "col"),
        P(("row", "col"), None, None),
        P(("row", "col"), None, None),
        P(("row", "col"), None, None),
        P("row", None, "col"),
        P("row", None, "col"),
        P("row", None),
        P("row", None),
        P(),
        P("row"),
        P(),
    )
    out_specs = P("row", "col")
    return jax.shard_map(body, mesh=mesh, in_specs=in_specs, out_specs=out_specs, check_vma=False)
```

time: 143 us -> 120 us (0.84)
  the two profiles are of different devices: /device:TPU:26 before, /device:TPU:8 now
where the time goes in v5:
time: 120 us
  Pallas kernels  116 us (97%)
  local copies, waits for them, and re-layouts  2.58 us (2%)
    pallas_call x1, Pallas kernels, run_experts(): pl.pallas_call(functools.partial(expert_kernel, rows, cols, groups), out_...  116 us

profile of v5, /device:TPU:8, one launch (start us, length us, event | category | flops | bytes accessed | tf_op | source)
XLA Modules:
  0.0 119.6 jit_solution(4112285437905764386)
XLA Ops:
  0.0 116.0 %shard_map.109 = (f32[160,128]{1,0:T(8,128)}, f32[16,128]{1,0:T(8,128)}, bf16[32,64,160]{2,1,0:T(8,128)(2,1)}, s32[1,128]{1,0:T(1,128)}) custom-call(bf16[160,128]{1,0:T(8,128)(2,1)} %bitcast.21, bf16[32,160]{1,0:T(8,128)(2,1)} %bitcast.22, bf16[32,160]{1,0:T(8,128)(2,1)} %bitcast.23, s32[6,128]{1,0:T(8,128)} %bitcast.24, f32[6,128]{1,0:T(8,128)} %bitcast.25, ...), custom_call_target="tpu_custom_call" | custom-call | tf_op jit(solution)/shard_map/pallas_call | solution.py:320
  116.0 0.0 copy-start.2
  116.0 1.1 slice.3
  117.1 0.0 copy-start.1
  117.1 0.0 copy-done.2
  117.1 0.7 copy-done.1
  117.8 0.0 copy-start
  117.8 0.1 broadcast_select_fusion
  117.8 0.8 copy-done
  118.7 0.9 fusion.2
  (2 shorter events, 0.0 us)
Async XLA Ops:
  116.0 1.1 copy-start.2
  117.1 0.7 copy-start.1
  117.8 0.9 copy-start

commit v6 on v5

--- a/solution.py
+++ b/solution.py
@@ -39,12 +39,12 @@
     rows, cols, groups,
     tok_ref, adp_down_ref, adp_up_ref, ids_ref, vals_ref, perm_ref, lengths_ref, req_ref,
     gate_hbm, up_hbm, down_hbm,
-    total_ref, low_total_ref, all_ref, adapter_ref,
-    full_ref, maps_ref, pick_ref, comb_ref, out_buf, in_buf, part_buf, back_buf,
+    total_ref, low_total_ref, up_all_ref, adapter_ref,
+    all_ref, full_ref, maps_ref, pick_ref, comb_ref, out_buf, in_buf, part_buf, back_buf,
     gate_ref, up_ref, down_ref, gate_t, up_t, down_t, gate_acc, up_acc, low_ref, share_part,
     sum_out, sum_in, low_out, low_in,
     own_sem, ring_send, ring_recv, row_send, row_recv, out_send, out_recv, back_send, back_recv,
-    sum_send, sum_recv, low_send, low_recv,
+    pass_send, pass_recv, sum_send, sum_recv, low_send, low_recv,
 ):
     me_r, me_c = lax.axis_index("row"), lax.axis_index("col")
     sides = (lax.rem(me_c + 1, cols), lax.rem(me_c + cols - 1, cols))
@@ -95,10 +95,31 @@
         at = full_ref.at[shard(way, step + 1)]
         return remote(at, at, ring_send.at[way, step], ring_recv.at[way, step], "col", sides[way])
 
-    def row_copy(away, owner):
+    pairs = rows // 2
+    partner = me_r + 1 - 2 * lax.rem(me_r, 2)
+
+    def owner_at(device, turn):
+        return lax.rem(device + rows - 2 * turn, rows)
+
+    def row_copy(turn, owner):
         at = all_ref.at[owner]
-        peer = lax.rem(me_r + away, rows)
-        return remote(maps_ref, at, row_send.at[away], row_recv.at[away], "row", peer)
+        peer = lax.rem(me_r + 2 * turn, rows)
+        return remote(maps_ref, at, row_send.at[turn], row_recv.at[turn], "row", peer)
+
+    def handing(turn):
+        at = all_ref.at[owner_at(me_r, turn)]
+        return remote(at, at, pass_send.at[turn], pass_recv.at[turn], "row", partner)
+
+    def handed(turn):
+        at = all_ref.at[owner_at(partner, turn)]
+        return remote(at, at, pass_send.at[turn], pass_recv.at[turn], "row", partner)
+
+    def each_pair(do):
+        def step(turn, carry):
+            do(turn)
+            return carry
+
+        lax.fori_loop(1, pairs, step, 0)
 
     def lanes(group):
         return pl.ds(group * width, width)
@@ -136,6 +157,7 @@
     )
     for copy in own:
         copy.start()
+    each_pair(lambda turn: row_copy(turn, me_r).start())
 
     turn_at = lax.broadcasted_iota(jnp.int32, (rows, count_tok), 0)
     peer_at = lax.rem(me_r + mixed(turn_at, rows), rows)
@@ -208,22 +230,26 @@
                 for part in range(groups):
                     tile = plain[:, part * width : (part + 1) * width]
                     turned[4 * part : 4 * part + 4] = tile.T.reshape(4, share, hidden_units)
-            each_turn(lambda turn: row_copy(mixed(turn, rows), me_r).start())
+    handing(0).start()
+
+    def hand_on(turn):
+        row_copy(turn, owner_at(me_r, turn)).wait_recv()
+        handing(turn).start()
+
+    each_pair(hand_on)
     for group in range(groups - 1):
         accumulate(group)
 
-    def row_end(away, carry):
-        row_copy(away, lax.rem(me_r + rows - away, rows)).wait_recv()
-        return carry
-
-    lax.fori_loop(1, rows, row_end, 0)
+    for turn in range(pairs):
+        handed(turn).wait_recv()
     rank = low_ref.shape[0]
     own_adapters = kept // rank
     low_ref[...] = jnp.zeros_like(low_ref)
 
     def project(owner, carry):
-        piece = all_ref[owner][:kept]
-        projected = contract(piece, tok_ref[...], 1, 0)
+        piece = all_ref[owner]
+        up_all_ref[owner] = piece[kept:]
+        projected = contract(piece[:kept], tok_ref[...], 1, 0)
         for i in range(own_adapters):
             chosen = adapter == owner * own_adapters + i
             low_ref[...] += jnp.where(chosen, projected[i * rank : (i + 1) * rank], 0.0)
@@ -294,7 +320,9 @@
         for step in range(sum_hops[way]):
             for copy in sums(way, step):
                 copy.wait_send()
-    each_turn(lambda turn: row_copy(turn, me_r).wait_send())
+    each_pair(lambda turn: row_copy(turn, me_r).wait_send())
+    for turn in range(pairs):
+        handing(turn).wait_send()
     for group in range(groups):
         each_turn(lambda turn: outward(group, turn).wait_send())
         each_turn(lambda turn: homeward(group, turn).wait_send())
@@ -322,12 +350,13 @@
         out_shape=(
             jax.ShapeDtypeStruct((share, count_tok), jnp.float32),
             jax.ShapeDtypeStruct((rank, count_tok), jnp.float32),
-            jax.ShapeDtypeStruct((rows,) + maps, jnp.bfloat16),
+            jax.ShapeDtypeStruct((rows,) + adp_up.shape, jnp.bfloat16),
             jax.ShapeDtypeStruct((1, count_tok), jnp.int32),
         ),
         in_specs=[VMEM] * 6 + [smem] * 2 + [hbm] * 3,
         out_specs=(VMEM,) * 4,
         scratch_shapes=[
+            pltpu.VMEM((rows,) + maps, jnp.bfloat16),
             pltpu.VMEM((cols, share, count_tok), jnp.bfloat16),
             pltpu.VMEM(maps, jnp.bfloat16),
             pltpu.VMEM((slots, count_tok), jnp.bfloat16),
@@ -347,10 +376,11 @@
             pltpu.SemaphoreType.DMA((5,)),
             pltpu.SemaphoreType.DMA((2, cols)),
             pltpu.SemaphoreType.DMA((2, cols)),
-            pltpu.SemaphoreType.DMA((rows,)),
-            pltpu.SemaphoreType.DMA((rows,)),
+            pltpu.SemaphoreType.DMA((rows // 2,)),
+            pltpu.SemaphoreType.DMA((rows // 2,)),
         ]
         + [pltpu.SemaphoreType.DMA((groups, rows))] * 4
+        + [pltpu.SemaphoreType.DMA((rows // 2,))] * 2
         + [pltpu.SemaphoreType.DMA((2, hops))] * 4,
         compiler_params=pltpu.CompilerParams(collective_id=0, has_side_effects=True),
     )(tokens_t, adp_down, adp_up, ids, vals, perm, lengths, req_adapter, gate, up, down)
@@ -379,11 +409,11 @@
     own_adapters = adp_down.shape[0]
     adapters = own_adapters * rows_count
 
-    total, low, maps, adapter = run_experts(
+    total, low, up_all, adapter = run_experts(
         capacity, tokens.T, adp_down, adp_up, expert_ids.T, gate_vals.T, perm[None],
         lengths, req_adapter, w_gate[0], w_up[0], w_down[0],
     )
-    up_all = maps[:, own_adapters * rank :].reshape(adapters * rank, share)
+    up_all = up_all.reshape(adapters * rank, share)
     chosen = jnp.arange(adapters, dtype=jnp.int32)[:, None, None] == adapter[None]
 
     low = low.astype(jnp.bfloat16)

time: 120 us -> 112 us (0.933)
  the two profiles are of different devices: /device:TPU:8 before, /device:TPU:32 now
where the time goes in v6:
time: 112 us
  Pallas kernels  107 us (96%)
  local copies, waits for them, and re-layouts  2.13 us (2%)
  matrix products  1.98 us (2%)
    pallas_call x1, Pallas kernels, run_experts(): pl.pallas_call(functools.partial(expert_kernel, rows, cols, groups), out_...  107 us

profile of v6, /device:TPU:32, one launch (start us, length us, event | category | flops | bytes accessed | tf_op | source)
XLA Modules:
  0.0 111.7 jit_solution(8928589125343346073)
XLA Ops:
  0.0 107.5 %shard_map.109 = (f32[160,128]{1,0:T(8,128)}, f32[16,128]{1,0:T(8,128)}, bf16[32,32,160]{2,1,0:T(8,128)(2,1)}, s32[1,128]{1,0:T(1,128)}) custom-call(bf16[160,128]{1,0:T(8,128)(2,1)} %bitcast.21, bf16[32,160]{1,0:T(8,128)(2,1)} %bitcast.22, bf16[32,160]{1,0:T(8,128)(2,1)} %bitcast.23, s32[6,128]{1,0:T(8,128)} %bitcast.24, f32[6,128]{1,0:T(8,128)} %bitcast.25, ...), custom_call_target="tpu_custom_call" | custom-call | tf_op jit(solution)/shard_map/pallas_call | solution.py:348
  107.5 0.0 copy-start.1
  107.5 0.7 copy-done.1
  108.2 0.0 copy-start.2
  108.2 0.6 copy-done.2
  108.8 0.0 copy-start
  108.8 0.1 broadcast_select_fusion
  108.9 0.8 copy-done
  109.7 2.0 %fusion.2 = bf16[128,160]{0,1:T(8,128)(2,1)} fusion(f32[160,128]{1,0:T(8,128)S(1)} %copy-done, bf16[1024,160]{1,0:T(8,128)(2,1)} %bitcast.20, bf16[1024,128]{1,0:T(8,128)(2,1)S(1)} %bitcast.16), kind=kOutput, calls=%fused_computation.3 | convolution fusion | flops 42004480 | bytes 712704 | tf_op jit(solution)/shard_map/dot_general | solution.py:18
  (2 shorter events, 0.0 us)
Async XLA Ops:
  107.5 0.7 copy-start.1
  108.2 0.6 copy-start.2
  108.8 0.9 copy-start

commit v7 on v6

--- a/solution.py
+++ b/solution.py
@@ -223,13 +223,6 @@
         out_buf[:, :, group * width : (group + 1) * width] = block
         in_buf[0, :, group * width : (group + 1) * width] = block[0]
         each_turn(lambda turn: outward(group, turn).start())
-        if group == 0:
-            for copy in weights:
-                copy.wait()
-            for plain, turned in ((gate_ref, gate_t), (up_ref, up_t), (down_ref, down_t)):
-                for part in range(groups):
-                    tile = plain[:, part * width : (part + 1) * width]
-                    turned[4 * part : 4 * part + 4] = tile.T.reshape(4, share, hidden_units)
     handing(0).start()
 
     def hand_on(turn):
@@ -237,6 +230,12 @@
         handing(turn).start()
 
     each_pair(hand_on)
+    for copy in weights:
+        copy.wait()
+    for plain, turned in ((gate_ref, gate_t), (up_ref, up_t), (down_ref, down_t)):
+        for part in range(groups):
+            tile = plain[:, part * width : (part + 1) * width]
+            turned[4 * part : 4 * part + 4] = tile.T.reshape(4, share, hidden_units)
     for group in range(groups - 1):
         accumulate(group)
 

time: 112 us -> 113 us (level)
  no operation moved by 1% of the time
where the time goes in v7:
time: 113 us; the launch traced here: 112 us
  Pallas kernels  108 us (96%)
  local copies, waits for them, and re-layouts  2.13 us (2%)
  matrix products  1.98 us (2%)
    pallas_call x1, Pallas kernels, run_experts(): pl.pallas_call(functools.partial(expert_kernel, rows, cols, groups), out_...  108 us

profile of v7, /device:TPU:32, one launch (start us, length us, event | category | flops | bytes accessed | tf_op | source)
XLA Modules:
  0.0 112.3 jit_solution(3224500489689407748)
XLA Ops:
  0.0 108.1 %shard_map.109 = (f32[160,128]{1,0:T(8,128)}, f32[16,128]{1,0:T(8,128)}, bf16[32,32,160]{2,1,0:T(8,128)(2,1)}, s32[1,128]{1,0:T(1,128)}) custom-call(bf16[160,128]{1,0:T(8,128)(2,1)} %bitcast.21, bf16[32,160]{1,0:T(8,128)(2,1)} %bitcast.22, bf16[32,160]{1,0:T(8,128)(2,1)} %bitcast.23, s32[6,128]{1,0:T(8,128)} %bitcast.24, f32[6,128]{1,0:T(8,128)} %bitcast.25, ...), custom_call_target="tpu_custom_call" | custom-call | tf_op jit(solution)/shard_map/pallas_call | solution.py:347
  108.1 0.0 copy-start.1
  108.1 0.7 copy-done.1
  108.8 0.0 copy-start.2
  108.8 0.6 copy-done.2
  109.5 0.0 copy-start
  109.5 0.1 broadcast_select_fusion
  109.5 0.8 copy-done
  110.4 2.0 %fusion.2 = bf16[128,160]{0,1:T(8,128)(2,1)} fusion(f32[160,128]{1,0:T(8,128)S(1)} %copy-done, bf16[1024,160]{1,0:T(8,128)(2,1)} %bitcast.20, bf16[1024,128]{1,0:T(8,128)(2,1)S(1)} %bitcast.16), kind=kOutput, calls=%fused_computation.3 | convolution fusion | flops 42004480 | bytes 712704 | tf_op jit(solution)/shard_map/dot_general | solution.py:18
  (2 shorter events, 0.0 us)
Async XLA Ops:
  108.1 0.7 copy-start.1
  108.8 0.6 copy-start.2
  109.5 0.9 copy-start
